TPU v7x, 32 devices: a whole 2x2x4 slice. The times are simulated.
32 devices in a mesh: dp: 16 (over z, y, x), mp: 2 (over core).
Axes of the slice: x: 2, y: 2, z: 4, core: 2. Of those that a mesh axis runs over, the one named last changes fastest.
Arguments:
- tokens: bfloat16 [32768, 384], P('dp'), may hold values from -6 to 6
- condition: bfloat16 [128, 384], P('dp'), may hold values from -6 to 6
- adaln_weight: bfloat16 [384, 2304], P('dp'), may hold values from -0.3125 to 0.3125
- adaln_bias: bfloat16 [6, 384], P(None, 'dp'), may hold values from -3 to 3
- qkv_weight: bfloat16 [3, 384, 384], P(None, 'dp', 'mp'), may hold values from -0.3125 to 0.3125
- qv_bias: bfloat16 [2, 2, 192], P(None, 'mp', 'dp'), may hold values from -3 to 3
- mix_weight: bfloat16 [384, 384], P('mp', 'dp'), may hold values from -1.25 to 1.25
- mix_bias: bfloat16 [384], P('dp'), may hold values from -3 to 3
- widen_weight: bfloat16 [384, 1536], P('dp', 'mp'), may hold values from -0.3125 to 0.3125
- widen_bias: bfloat16 [2, 768], P('mp', 'dp'), may hold values from -3 to 3
- narrow_weight: bfloat16 [1536, 384], P('mp', 'dp'), may hold values from -0.15625 to 0.15625
- narrow_bias: bfloat16 [384], P('dp'), may hold values from -3 to 3
- cotangent: bfloat16 [32768, 384], P('dp'), may hold values from -6 to 6
Outputs:
- block_out: bfloat16 [32768, 384], P('dp')
- tokens_grad: bfloat16 [32768, 384], P('dp')
- condition_grad: bfloat16 [128, 384], P('dp')
- adaln_weight_grad: float32 [384, 2304], P('dp')
- adaln_bias_grad: float32 [6, 384], P(None, 'dp')
- qkv_weight_grad: float32 [3, 384, 384], P(None, 'dp', 'mp')
- qv_bias_grad: float32 [2, 2, 192], P(None, 'mp', 'dp')
- mix_weight_grad: float32 [384, 384], P('mp', 'dp')
- mix_bias_grad: float32 [384], P('dp')
- expand_weight_grad: float32 [384, 1536], P('dp', 'mp')
- expand_bias_grad: float32 [2, 768], P('mp', 'dp')
- reduce_weight_grad: float32 [1536, 384], P('mp', 'dp')
- reduce_bias_grad: float32 [384], P('dp')
All inputs are finite; a program needn't handle non-finite values.
Results may differ from a plain program's by a relative error of at most 0.015.
Values may be sent and summed in bfloat16 or wider, within the bound.
No kernel may reach another device: no remote copies, remote signals or barrier semaphores. Data moves between devices by JAX's collectives and lax.ppermute only.
A program may use at most 128 MiB of HBM per device.

v0:
```python
import jax
import jax.numpy as jnp
from jax import lax
from jax.sharding import PartitionSpec as P

HEAD_DIM = 64


EPS = 1e-06


def in_blocks(array, dim, size):
    before, after = (array.shape[:dim], array.shape[dim + 1 :])
    return jnp.moveaxis(array.reshape(*before, size, -1, *after), dim, 0)


def sent_and_summed(array, axis, dim):
    blocks = in_blocks(array, dim, lax.axis_size(axis))
    arrived = lax.all_to_all(blocks, axis, split_axis=0, concat_axis=0, tiled=True)
    return arrived.astype(jnp.float32).sum(axis=0)


def sent_together(arrays, axis, dim, along):
    columns = [a.reshape(*a.shape[:along], -1) for a in arrays]
    both = jnp.concatenate(columns, axis=along)
    result, at, finished = (sent_and_summed(both, axis, dim), 0, [])
    for a, column in zip(arrays, columns):
        share = result[..., at : at + column.shape[along]]
        finished.append(share.reshape(*share.shape[:along], *a.shape[along:]))
        at += column.shape[along]
    return tuple(finished)


def silu_act(inputs):
    return inputs * jax.nn.sigmoid(inputs)


def gelu_tanh(inputs):
    return (
        0.5
        * inputs
        * (1.0 + jnp.tanh(0.7978845608028654 * (inputs + 0.044715 * inputs * inputs * inputs)))
    )


def normalize(inputs):
    centered = inputs - jnp.mean(inputs, axis=-1, keepdims=True)
    return centered * lax.rsqrt(jnp.mean(centered * centered, axis=-1, keepdims=True) + EPS)


def modulate(inputs, shift, scale):
    return normalize(inputs) * (1.0 + scale) + shift


def body(
    tokens,
    condition,
    adaln_weight,
    adaln_bias,
    qkv_weight,
    qv_bias,
    mix_weight,
    mix_bias,
    widen_weight,
    widen_bias,
    narrow_weight,
    narrow_bias,
    cotangent,
):
    gathered = (
        lax.all_gather(adaln_weight, "dp", axis=0, tiled=True),
        lax.all_gather(adaln_bias, "dp", axis=1, tiled=True),
        lax.all_gather(qkv_weight, "dp", axis=1, tiled=True),
        lax.all_gather(qv_bias, "dp", axis=2, tiled=True),
        lax.all_gather(mix_weight, "dp", axis=1, tiled=True),
        lax.all_gather(mix_bias, "dp", axis=0, tiled=True),
        lax.all_gather(widen_weight, "dp", axis=0, tiled=True),
        lax.all_gather(widen_bias, "dp", axis=1, tiled=True),
        lax.all_gather(narrow_weight, "dp", axis=1, tiled=True),
        lax.all_gather(narrow_bias, "dp", axis=0, tiled=True),
    )
    (
        full_adaln,
        full_adaln_bias,
        full_qkv,
        full_qv_bias,
        full_mix,
        full_mix_bias,
        full_expand,
        full_expand_bias,
        full_reduce,
        full_reduce_bias,
    ) = gathered
    latents = condition.shape[0]
    row_count = tokens.shape[0]
    seq_len = row_count // latents
    model_width = tokens.shape[1]
    local_width = qkv_weight.shape[2]
    local_heads = local_width // HEAD_DIM
    scale_qk = HEAD_DIM ** (-0.5)
    cond_float = condition.astype(jnp.float32)
    cond_act = silu_act(cond_float).astype(jnp.bfloat16)
    modulation = jnp.dot(
        cond_act, full_adaln, preferred_element_type=jnp.float32
    ) + full_adaln_bias.astype(jnp.float32).reshape(-1)
    pieces = modulation.reshape(latents, 6, 1, model_width)
    shift_one = pieces[:, 0]
    scale_one = pieces[:, 1]
    gate_one = pieces[:, 2]
    shift_two = pieces[:, 3]
    scale_two = pieces[:, 4]
    gate_two = pieces[:, 5]
    inputs = tokens.astype(jnp.float32).reshape(latents, seq_len, model_width)
    normed_one = (
        modulate(inputs, shift_one, scale_one).astype(jnp.bfloat16).reshape(row_count, model_width)
    )
    qv_float = full_qv_bias.astype(jnp.float32).reshape(2, local_width)
    bias_three = jnp.concatenate(
        [qv_float[:1], jnp.zeros((1, local_width), jnp.float32), qv_float[1:]], axis=0
    )
    projected = (
        jnp.einsum("td,jde->jte", normed_one, full_qkv, preferred_element_type=jnp.float32)
        + bias_three[:, None, :]
    )
    projected = projected.astype(jnp.bfloat16)
    head_view = projected.reshape(3, latents, seq_len, local_heads, HEAD_DIM)
    query_h = head_view[0]
    key_h = head_view[1]
    value_h = head_view[2]
    scores = (
        jnp.einsum("lqhd,lkhd->lhqk", query_h, key_h, preferred_element_type=jnp.float32) * scale_qk
    )
    row_max = jnp.max(scores, axis=-1, keepdims=True)
    exp_scores = jnp.exp(scores - row_max)
    denom_sum = jnp.sum(exp_scores, axis=-1, keepdims=True)
    attn_prob = exp_scores / denom_sum
    log_total = row_max + jnp.log(denom_sum)
    attended = jnp.einsum(
        "lhqk,lkhd->lqhd",
        attn_prob.astype(jnp.bfloat16),
        value_h,
        preferred_element_type=jnp.float32,
    )
    attended = attended.astype(jnp.bfloat16).reshape(row_count, local_width)
    attn_part = jnp.dot(attended, full_mix, preferred_element_type=jnp.float32)
    attn_branch = lax.psum(attn_part.astype(jnp.bfloat16), "mp").astype(
        jnp.float32
    ) + full_mix_bias.astype(jnp.float32)
    attn_branch = attn_branch.reshape(latents, seq_len, model_width)
    middle = inputs + gate_one * attn_branch
    second_normed = (
        modulate(middle, shift_two, scale_two).astype(jnp.bfloat16).reshape(row_count, model_width)
    )
    before_activation = jnp.dot(
        second_normed, full_expand, preferred_element_type=jnp.float32
    ) + full_expand_bias.astype(jnp.float32).reshape(-1)
    activated_hidden = gelu_tanh(before_activation).astype(jnp.bfloat16)
    mlp_part = jnp.dot(activated_hidden, full_reduce, preferred_element_type=jnp.float32)
    feedforward_branch = lax.psum(mlp_part.astype(jnp.bfloat16), "mp").astype(
        jnp.float32
    ) + full_reduce_bias.astype(jnp.float32)
    feedforward_branch = feedforward_branch.reshape(latents, seq_len, model_width)
    block_out = (
        (middle + gate_two * feedforward_branch)
        .astype(jnp.bfloat16)
        .reshape(row_count, model_width)
    )
    back_adaln, back_qkv, back_mix, back_expand, back_reduce = (
        full_adaln,
        full_qkv,
        full_mix,
        full_expand,
        full_reduce,
    )
    upstream = cotangent.astype(jnp.float32).reshape(latents, seq_len, model_width)
    mlp_grad = (gate_two * upstream).astype(jnp.bfloat16).reshape(row_count, model_width)
    gate_two_grad = jnp.sum(upstream * feedforward_branch, axis=1)
    reduce_bias_grad = jnp.sum(mlp_grad, axis=0, dtype=jnp.float32)
    reduce_grad = jnp.einsum(
        "tf,td->fd", activated_hidden, mlp_grad, preferred_element_type=jnp.float32
    )
    act_grad = jnp.einsum("td,fd->tf", mlp_grad, back_reduce, preferred_element_type=jnp.float32)
    gelu_back = jax.vjp(gelu_tanh, before_activation)[1]
    pre_grad = gelu_back(act_grad)[0].astype(jnp.bfloat16)
    expand_bias_grad = jnp.sum(pre_grad, axis=0, dtype=jnp.float32).reshape(1, -1)
    expand_grad = jnp.einsum(
        "td,tf->df", second_normed, pre_grad, preferred_element_type=jnp.float32
    )
    normed_two_part = jnp.einsum(
        "tf,df->td", pre_grad, back_expand, preferred_element_type=jnp.float32
    )
    normed_two_grad = (
        lax.psum(normed_two_part.astype(jnp.bfloat16), "mp")
        .astype(jnp.float32)
        .reshape(latents, seq_len, model_width)
    )
    second_back = jax.vjp(modulate, middle, shift_two, scale_two)[1]
    middle_ln_grad, shift_lat_two, scale_lat_two = second_back(normed_two_grad)
    shift_two_grad = shift_lat_two[:, 0]
    scale_two_grad = scale_lat_two[:, 0]
    middle_grad = upstream + middle_ln_grad
    gate_one_grad = jnp.sum(middle_grad * attn_branch, axis=1)
    attn_grad = (gate_one * middle_grad).astype(jnp.bfloat16).reshape(row_count, model_width)
    mix_bias_grad = jnp.sum(attn_grad, axis=0, dtype=jnp.float32)
    mix_grad = jnp.einsum("te,td->ed", attended, attn_grad, preferred_element_type=jnp.float32)
    attended_grad = jnp.einsum("td,ed->te", attn_grad, back_mix, preferred_element_type=jnp.float32)
    attended_grad = attended_grad.astype(jnp.bfloat16).reshape(
        latents, seq_len, local_heads, HEAD_DIM
    )
    scores_again = (
        jnp.einsum("lqhd,lkhd->lhqk", query_h, key_h, preferred_element_type=jnp.float32) * scale_qk
    )
    prob_again = jnp.exp(scores_again - log_total)
    prob_grad = jnp.einsum(
        "lqhd,lkhd->lhqk", attended_grad, value_h, preferred_element_type=jnp.float32
    )
    value_grad = jnp.einsum(
        "lhqk,lqhd->lkhd",
        prob_again.astype(jnp.bfloat16),
        attended_grad,
        preferred_element_type=jnp.float32,
    ).astype(jnp.bfloat16)
    row_inner = jnp.sum(prob_again * prob_grad, axis=-1, keepdims=True)
    score_grad = (prob_again * (prob_grad - row_inner)).astype(jnp.bfloat16)
    query_grad = (
        jnp.einsum("lhqk,lkhd->lqhd", score_grad, key_h, preferred_element_type=jnp.float32)
        * scale_qk
    ).astype(jnp.bfloat16)
    key_grad = (
        jnp.einsum("lhqk,lqhd->lkhd", score_grad, query_h, preferred_element_type=jnp.float32)
        * scale_qk
    ).astype(jnp.bfloat16)
    qkv_out_grad = jnp.stack([query_grad, key_grad, value_grad]).reshape(3, row_count, local_width)
    qv_bias_grad = jnp.stack(
        [
            jnp.sum(qkv_out_grad[0], axis=0, dtype=jnp.float32),
            jnp.sum(qkv_out_grad[2], axis=0, dtype=jnp.float32),
        ]
    ).reshape(2, 1, local_width)
    qkv_grad = jnp.einsum(
        "td,jte->jde", normed_one, qkv_out_grad, preferred_element_type=jnp.float32
    )
    normed_one_part = jnp.einsum(
        "jte,jde->td", qkv_out_grad, back_qkv, preferred_element_type=jnp.float32
    )
    normed_one_grad = (
        lax.psum(normed_one_part.astype(jnp.bfloat16), "mp")
        .astype(jnp.float32)
        .reshape(latents, seq_len, model_width)
    )
    first_back = jax.vjp(modulate, inputs, shift_one, scale_one)[1]
    inputs_ln_grad, shift_lat_one, scale_lat_one = first_back(normed_one_grad)
    tokens_grad = (
        (middle_grad + inputs_ln_grad).astype(jnp.bfloat16).reshape(row_count, model_width)
    )
    six_grads = (
        shift_lat_one[:, 0],
        scale_lat_one[:, 0],
        gate_one_grad,
        shift_two_grad,
        scale_two_grad,
        gate_two_grad,
    )
    mod_grad = jnp.stack(tuple(six_grads), axis=1)
    mod_grad = mod_grad.astype(jnp.bfloat16).reshape(latents, 6 * model_width)
    adaln_bias_grad = jnp.sum(mod_grad, axis=0, dtype=jnp.float32).reshape(6, model_width)
    adaln_grad = jnp.einsum("ld,le->de", cond_act, mod_grad, preferred_element_type=jnp.float32)
    cond_act_grad = jnp.einsum(
        "le,de->ld", mod_grad, back_adaln, preferred_element_type=jnp.float32
    )
    silu_back = jax.vjp(silu_act, cond_float)[1]
    condition_grad = silu_back(cond_act_grad)[0].astype(jnp.bfloat16)
    summed = (
        sent_and_summed(adaln_grad.astype(jnp.bfloat16), "dp", 0),
        sent_and_summed(adaln_bias_grad.astype(jnp.bfloat16), "dp", 1),
        sent_and_summed(qkv_grad.astype(jnp.bfloat16), "dp", 1),
        sent_and_summed(qv_bias_grad.astype(jnp.bfloat16), "dp", 2),
        sent_and_summed(mix_grad.astype(jnp.bfloat16), "dp", 1),
        *sent_together(
            (mix_bias_grad.astype(jnp.bfloat16), expand_grad.astype(jnp.bfloat16)), "dp", 0, 1
        ),
        sent_and_summed(expand_bias_grad.astype(jnp.bfloat16), "dp", 1),
        sent_and_summed(reduce_grad.astype(jnp.bfloat16), "dp", 1),
        sent_and_summed(reduce_bias_grad.astype(jnp.bfloat16), "dp", 0),
    )
    return (
        block_out,
        tokens_grad,
        condition_grad,
        summed[0],
        summed[1],
        summed[2],
        summed[3],
        summed[4],
        summed[5],
        summed[6],
        summed[7],
        summed[8],
        summed[9],
    )


def solution(mesh):
    return jax.shard_map(
        body,
        mesh=mesh,
        in_specs=(
            P("dp", None),
            P("dp", None),
            P("dp", None),
            P(None, "dp"),
            P(None, "dp", "mp"),
            P(None, "mp", "dp"),
            P("mp", "dp"),
            P("dp"),
            P("dp", "mp"),
            P("mp", "dp"),
            P("mp", "dp"),
            P("dp"),
            P("dp", None),
        ),
        out_specs=(
            P("dp", None),
            P("dp", None),
            P("dp", None),
            P("dp", None),
            P(None, "dp"),
            P(None, "dp", "mp"),
            P(None, "mp", "dp"),
            P("mp", "dp"),
            P("dp"),
            P("dp", "mp"),
            P("mp", "dp"),
            P("mp", "dp"),
            P("dp"),
        ),
        check_vma=False,
    )
```

profile of v0, /device:TPU:12, one launch (start us, length us, event | category | flops | bytes accessed | tf_op | source)
XLA Modules:
  0.0 568.6 jit_solution(11415103758796047594)
XLA Ops:
  8.7 31.4 %all-gather = bf16[16,24,6]{1,2,0:T(8,128)(2,1)S(1)} all-gather(bf16[1,24,6]{1,2,0:T(8,128)(2,1)} %bitcast.265), channel_id=1, replica_groups=mesh['dp'=16,'mp'=2] {'dp'}, dimensions={0}, use_global_device_ids=true | all-gather | bytes 4896 | tf_op jit(solution)/shard_map/all_gather | solution.py:72
  40.2 36.6 %all_gather.33 = bf16[2,1,192]{1,0,2:T(2,128)(2,1)S(1)} all-gather(bf16[2,1,12]{1,0,2:T(2,128)(2,1)S(1)} %copy.167), channel_id=1, replica_groups=mesh['dp'=16,'mp'=2] {'dp'}, dimensions={2}, use_global_device_ids=true | all-gather | bytes 816 | tf_op jit(solution)/shard_map/all_gather | solution.py:74
  77.0 38.7 %all_gather.34 = bf16[192,384]{0,1:T(8,128)(2,1)S(1)} all-gather(bf16[192,24]{0,1:T(8,128)(2,1)} %param.19), channel_id=1, replica_groups=mesh['dp'=16,'mp'=2] {'dp'}, dimensions={1}, use_global_device_ids=true | all-gather | bytes 156672 | tf_op jit(solution)/shard_map/all_gather | solution.py:75
  118.5 39.6 %all_gather.32 = bf16[3,384,192]{2,1,0:T(8,128)(2,1)S(1)} all-gather(bf16[3,24,192]{2,1,0:T(8,128)(2,1)} %param.17), channel_id=1, replica_groups=mesh['dp'=16,'mp'=2] {'dp'}, dimensions={1}, use_global_device_ids=true | all-gather | bytes 470016 | tf_op jit(solution)/shard_map/all_gather | solution.py:73
  175.7 38.8 %all-reduce.3 = (bf16[384]{0:T(512)(128)(2,1)}, bf16[384]{0:T(512)(128)(2,1)S(1)}, bf16[768]{0:T(1024)(128)(2,1)S(1)}) all-reduce(bf16[384]{0:T(512)(128)(2,1)S(1)} %dynamic-update-slice.2, bf16[384]{0:T(512)(128)(2,1)S(1)} %dynamic-update-slice, bf16[768]{0:T(1024)(128)(2,1)S(1)} %dynamic-update-slice.1), channel_id=1, replica_groups=mesh['dp'=16,'mp'=2] {'dp'}, use_global_device_ids=true, to_apply=%add.2 | all-reduce | flops 1536 | bytes 6144
  214.4 42.0 %all_gather.36 = bf16[384,768]{1,0:T(8,128)(2,1)} all-gather(bf16[24,768]{1,0:T(8,128)(2,1)} %param.21), channel_id=1, replica_groups=mesh['dp'=16,'mp'=2] {'dp'}, dimensions={0}, use_global_device_ids=true | all-gather | bytes 626688 | tf_op jit(solution)/shard_map/all_gather | solution.py:77
  256.5 43.3 %all_gather.38 = bf16[768,384]{0,1:T(8,128)(2,1)} all-gather(bf16[768,24]{0,1:T(8,128)(2,1)} %param.23), channel_id=1, replica_groups=mesh['dp'=16,'mp'=2] {'dp'}, dimensions={1}, use_global_device_ids=true | all-gather | bytes 626688 | tf_op jit(solution)/shard_map/all_gather | solution.py:79
  310.5 7.0 %fusion.86 = (bf16[768]{0:T(1024)(128)(2,1)}, bf16[2048,768]{1,0:T(8,128)(2,1)S(1)}) fusion(bf16[2048,384]{1,0:T(8,128)(2,1)S(1)} %copy-done.24, bf16[768,384]{0,1:T(8,128)(2,1)S(1)} %copy-done.27, f32[2048,768]{1,0:T(8,128)S(1)} %get-tuple-element.141, f32[768]{0:T(1024)S(1)} %add.236), kind=kOutput, calls=%fused_computation.168 | convolution fusion | flops 1248853248 | bytes 11604480 | tf_op jit(solution)/shard_map/td,fd->tf/dot_general | solution.py:182
  322.3 5.0 convolution_convert_fusion.2
  327.2 21.8 %all-reduce.11.cloned.1.call-done = bf16[2048,384]{1,0:T(8,128)(2,1)} async-done(((bf16[2048,384]{1,0:T(8,128)(2,1)}), bf16[2048,384]{1,0:T(8,128)(2,1)}) %all-reduce.11.cloned.1.call-update) | async-done | bytes 1572880 | tf_op jit(solution)/shard_map/psum | solution.py:193
  392.7 7.0 %all-to-all-start.8 = ((bf16[16,1,24]{2,1,0:T(2,128)(2,1)}), bf16[16,1,24]{2,1,0:T(2,128)(2,1)S(1)}, u32[]{:S(2)}, u32[]{:S(2)}) async-start(bf16[16,1,24]{2,1,0:T(2,128)(2,1)} %all_to_all.40), calls=%async_computation.8 | async-start | bytes 16384 | tf_op jit(solution)/shard_map/all_to_all | solution.py:19
  404.7 5.6 all-to-all-start.6
  410.3 5.1 convolution_convert_fusion.5
  416.0 7.0 %all-to-all-start.7 = ((bf16[16,768,24]{1,2,0:T(8,128)(2,1)}), bf16[16,768,24]{1,2,0:T(8,128)(2,1)}, u32[]{:S(2)}, u32[]{:S(2)}) async-start(bf16[16,768,24]{1,2,0:T(8,128)(2,1)} %bitcast.256), calls=%async_computation.7 | async-start | bytes 1179648 | tf_op jit(solution)/shard_map/all_to_all | solution.py:19
  424.5 12.3 %all-to-all-done.7 = bf16[16,768,24]{1,2,0:T(8,128)(2,1)} async-done(((bf16[16,768,24]{1,2,0:T(8,128)(2,1)}), bf16[16,768,24]{1,2,0:T(8,128)(2,1)}, u32[]{:S(2)}, u32[]{:S(2)}) %all-to-all-start.7) | async-done | bytes 589856 | tf_op jit(solution)/shard_map/all_to_all | solution.py:19
  436.8 5.1 all-to-all-start.3
  446.8 5.7 all-to-all-start.4
  460.8 7.0 %all-to-all-start.2 = ((bf16[16,3,24,192]{3,2,1,0:T(8,128)(2,1)}), bf16[16,3,24,192]{3,2,1,0:T(8,128)(2,1)}, u32[]{:S(2)}, u32[]{:S(2)}) async-start(bf16[16,3,24,192]{3,2,1,0:T(8,128)(2,1)} %copy.186), calls=%async_computation.2 | async-start | bytes 1179648 | tf_op jit(solution)/shard_map/all_to_all | solution.py:19
  476.9 6.0 %fusion.27 = (bf16[8,384]{1,0:T(8,128)(2,1)S(1)}, bf16[8,384]{1,0:T(8,128)(2,1)S(1)}, bf16[8,384]{1,0:T(8,128)(2,1)S(1)}, bf16[8,384]{1,0:T(8,128)(2,1)S(1)}, bf...) fusion(bf16[2048,384]{1,0:T(8,128)(2,1)} %all-reduce.11.cloned.1.call-done, bf16[2048,384]{1,0:T(8,128)(2,1)S(1)} %copy-done.2, ...), kind=kLoop, calls=%fused_computation.56 | loop fusion | flops 24360960 | bytes 9550848 | tf_op jit(solution)/shard_map/transpose(jvp())/reduce_sum | solution.py:52
  482.9 6.9 %all-to-all-start.5 = ((bf16[16,24,769]{2,1,0:T(8,128)(2,1)}), bf16[16,24,769]{2,1,0:T(8,128)(2,1)}, u32[]{:S(2)}, u32[]{:S(2)}) async-start(bf16[16,24,769]{2,1,0:T(8,128)(2,1)} %pad_maximum_fusion), calls=%async_computation.5 | async-start | bytes 1376256 | tf_op jit(solution)/shard_map/all_to_all | solution.py:19
  490.7 12.9 %all-to-all-done.5 = bf16[16,24,769]{2,1,0:T(8,128)(2,1)} async-done(((bf16[16,24,769]{2,1,0:T(8,128)(2,1)}), bf16[16,24,769]{2,1,0:T(8,128)(2,1)}, u32[]{:S(2)}, u32[]{:S(2)}) %all-to-all-start.5) | async-done | bytes 590624 | tf_op jit(solution)/shard_map/all_to_all | solution.py:19
  503.6 5.1 all-to-all-start.1
  513.9 6.8 %all-to-all-start = ((bf16[16,24,2304]{2,1,0:T(8,128)(2,1)}), bf16[16,24,2304]{2,1,0:T(8,128)(2,1)}, u32[]{:S(2)}, u32[]{:S(2)}) async-start(bf16[16,24,2304]{2,1,0:T(8,128)(2,1)} %bitcast.243), calls=%async_computation | async-start | bytes 3538944 | tf_op jit(solution)/shard_map/all_to_all | solution.py:19
  537.7 21.5 %all-to-all-done = bf16[16,24,2304]{2,1,0:T(8,128)(2,1)} async-done(((bf16[16,24,2304]{2,1,0:T(8,128)(2,1)}), bf16[16,24,2304]{2,1,0:T(8,128)(2,1)}, u32[]{:S(2)}, u32[]{:S(2)}) %all-to-all-start) | async-done | bytes 1769504 | tf_op jit(solution)/shard_map/all_to_all | solution.py:19
  (233 shorter events, 134.2 us)
Async XLA Ops:
  7.2 151.0 %copy-start = (bf16[2048,384]{1,0:T(8,128)(2,1)S(1)}, bf16[2048,384]{1,0:T(8,128)(2,1)}, u32[]{:S(2)}) copy-start(bf16[2048,384]{1,0:T(8,128)(2,1)} %param.13) | copy-start | bytes 4718596
  7.2 151.9 %copy-start.32 = (bf16[8,384]{1,0:T(8,128)(2,1)S(1)}, bf16[8,384]{1,0:T(8,128)(2,1)}, u32[]{:S(2)}) copy-start(bf16[8,384]{1,0:T(8,128)(2,1)} %param.14) | copy-start | bytes 18436
  7.2 151.9 %all-gather.3.cloned.1.call-start = ((), (), s32[]{:S(2)}) async-start(), calls=%async_computation.9 | async-start | bytes 1880064 | tf_op jit(solution)/shard_map/all_gather | solution.py:71
  7.9 293.4 %all-reduce.9.cloned.1.call-start = ((), (), s32[]{:S(2)}) async-start(), calls=%async_computation.10 | async-start | bytes 3145728 | tf_op jit(solution)/shard_map/psum | solution.py:146
  169.9 129.8 %copy-start.6 = (bf16[2048,384]{1,0:T(8,128)(2,1)S(1)}, bf16[2048,384]{1,0:T(8,128)(2,1)}, u32[]{:S(2)}) copy-start(bf16[2048,384]{1,0:T(8,128)(2,1)} %param.25) | copy-start | bytes 4718596
  173.0 176.0 %all-reduce.11.cloned.1.call-start = ((), (), s32[]{:S(2)}) async-start(), calls=%async_computation.11 | async-start | bytes 3145728 | tf_op jit(solution)/shard_map/psum | solution.py:193
  322.2 154.7 %all-reduce.13.cloned.1.call-start = ((), (), s32[]{:S(2)}) async-start(), calls=%async_computation.12 | async-start | bytes 6291456 | tf_op jit(solution)/shard_map/psum | solution.py:159
  392.7 11.9 %all-to-all-start.8 = ((bf16[16,1,24]{2,1,0:T(2,128)(2,1)}), bf16[16,1,24]{2,1,0:T(2,128)(2,1)S(1)}, u32[]{:S(2)}, u32[]{:S(2)}) async-start(bf16[16,1,24]{2,1,0:T(2,128)(2,1)} %all_to_all.40), calls=%async_computation.8 | async-start | bytes 16384 | tf_op jit(solution)/shard_map/all_to_all | solution.py:19
  404.7 10.7 %copy-start.35 = (bf16[16,1,24]{2,1,0:T(2,128)(2,1)}, bf16[16,1,24]{2,1,0:T(2,128)(2,1)S(1)}, u32[]{:S(2)}) copy-start(bf16[16,1,24]{2,1,0:T(2,128)(2,1)S(1)} %all-to-all-done.8) | copy-start | bytes 2308
  404.7 10.7 %all-to-all-start.6 = ((bf16[16,1,48]{2,1,0:T(2,128)(2,1)}), bf16[16,1,48]{2,1,0:T(2,128)(2,1)S(1)}, u32[]{:S(2)}, u32[]{:S(2)}) async-start(bf16[16,1,48]{2,1,0:T(2,128)(2,1)} %convert_element_type.280), calls=%async_computation.6 | async-start | bytes 16384 | tf_op jit(solution)/shard_map/all_to_all | solution.py:19
  410.3 12.7 %copy-start.42 = (bf16[384]{0:T(512)(128)(2,1)S(1)}, bf16[384]{0:T(512)(128)(2,1)}, u32[]{:S(2)}) copy-start(bf16[384]{0:T(512)(128)(2,1)} %get-tuple-element.112) | copy-start | bytes 2308
  410.3 12.7 %copy-start.34 = (f32[2048]{0:T(1024)S(1)}, f32[2048]{0:T(1024)}, u32[]{:S(2)}) copy-start(f32[2048]{0:T(1024)} %get-tuple-element.136) | copy-start | bytes 24580
  416.0 20.8 %all-to-all-start.7 = ((bf16[16,768,24]{1,2,0:T(8,128)(2,1)}), bf16[16,768,24]{1,2,0:T(8,128)(2,1)}, u32[]{:S(2)}, u32[]{:S(2)}) async-start(bf16[16,768,24]{1,2,0:T(8,128)(2,1)} %bitcast.256), calls=%async_computation.7 | async-start | bytes 1179648 | tf_op jit(solution)/shard_map/all_to_all | solution.py:19
  436.8 10.0 %all-to-all-start.3 = ((bf16[16,2,1,12]{3,1,2,0:T(2,128)(2,1)}), bf16[16,2,1,12]{3,1,2,0:T(2,128)(2,1)S(1)}, u32[]{:S(2)}, u32[]{:S(2)}) async-start(bf16[16,2,1,12]{3,1,2,0:T(2,128)(2,1)} %copy.187), calls=%async_computation.3 | async-start | bytes 16384 | tf_op jit(solution)/shard_map/all_to_all | solution.py:19
  446.8 10.0 %copy-start.39 = (bf16[16,2,1,12]{3,1,2,0:T(2,128)(2,1)}, bf16[16,2,1,12]{3,1,2,0:T(2,128)(2,1)S(1)}, u32[]{:S(2)}) copy-start(bf16[16,2,1,12]{3,1,2,0:T(2,128)(2,1)S(1)} %all-to-all-done.3) | copy-start | bytes 2308
  446.8 14.0 %all-to-all-start.4 = ((bf16[16,192,24]{1,2,0:T(8,128)(2,1)}), bf16[16,192,24]{1,2,0:T(8,128)(2,1)S(1)}, u32[]{:S(2)}, u32[]{:S(2)}) async-start(bf16[16,192,24]{1,2,0:T(8,128)(2,1)} %bitcast.49), calls=%async_computation.4 | async-start | bytes 393216 | tf_op jit(solution)/shard_map/all_to_all | solution.py:19
  460.8 22.1 %all-to-all-start.2 = ((bf16[16,3,24,192]{3,2,1,0:T(8,128)(2,1)}), bf16[16,3,24,192]{3,2,1,0:T(8,128)(2,1)}, u32[]{:S(2)}, u32[]{:S(2)}) async-start(bf16[16,3,24,192]{3,2,1,0:T(8,128)(2,1)} %copy.186), calls=%async_computation.2 | async-start | bytes 1179648 | tf_op jit(solution)/shard_map/all_to_all | solution.py:19
  476.9 31.8 %copy-start.33 = (bf16[8,384]{1,0:T(8,128)(2,1)S(1)}, bf16[8,384]{1,0:T(8,128)(2,1)}, u32[]{:S(2)}) copy-start(bf16[8,384]{1,0:T(8,128)(2,1)} %param.14) | copy-start | bytes 18436
  482.9 20.7 %all-to-all-start.5 = ((bf16[16,24,769]{2,1,0:T(8,128)(2,1)}), bf16[16,24,769]{2,1,0:T(8,128)(2,1)}, u32[]{:S(2)}, u32[]{:S(2)}) async-start(bf16[16,24,769]{2,1,0:T(8,128)(2,1)} %pad_maximum_fusion), calls=%async_computation.5 | async-start | bytes 1376256 | tf_op jit(solution)/shard_map/all_to_all | solution.py:19
  489.9 30.9 %copy-start.36 = (bf16[16,1,24]{2,1,0:T(2,128)(2,1)S(1)}, bf16[16,1,24]{2,1,0:T(2,128)(2,1)}, u32[]{:S(2)}) copy-start(bf16[16,1,24]{2,1,0:T(2,128)(2,1)} %copy-done.35) | copy-start | bytes 2308
  489.9 31.5 %copy-start.38 = (bf16[16,1,48]{2,1,0:T(2,128)(2,1)S(1)}, bf16[16,1,48]{2,1,0:T(2,128)(2,1)}, u32[]{:S(2)}) copy-start(bf16[16,1,48]{2,1,0:T(2,128)(2,1)} %copy-done.37) | copy-start | bytes 4612
  489.9 33.8 %copy-start.40 = (bf16[16,2,1,12]{3,1,2,0:T(2,128)(2,1)S(1)}, bf16[16,2,1,12]{3,1,2,0:T(2,128)(2,1)}, u32[]{:S(2)}) copy-start(bf16[16,2,1,12]{3,1,2,0:T(2,128)(2,1)} %copy-done.39) | copy-start | bytes 2308
  503.6 10.3 %all-to-all-start.1 = ((bf16[16,6,24]{2,1,0:T(8,128)(2,1)}), bf16[16,6,24]{2,1,0:T(8,128)(2,1)S(1)}, u32[]{:S(2)}, u32[]{:S(2)}) async-start(bf16[16,6,24]{2,1,0:T(8,128)(2,1)} %copy.184), calls=%async_computation.1 | async-start | bytes 65536 | tf_op jit(solution)/shard_map/all_to_all | solution.py:19
  513.9 45.3 %all-to-all-start = ((bf16[16,24,2304]{2,1,0:T(8,128)(2,1)}), bf16[16,24,2304]{2,1,0:T(8,128)(2,1)}, u32[]{:S(2)}, u32[]{:S(2)}) async-start(bf16[16,24,2304]{2,1,0:T(8,128)(2,1)} %bitcast.243), calls=%async_computation | async-start | bytes 3538944 | tf_op jit(solution)/shard_map/all_to_all | solution.py:19
  (39 other events, 127.2 us)
Sparse Core Ops, SparseCore 0:
  10.8 59.4 all-gather.2
  173.1 27.7 all-reduce.8
  322.3 26.6 all-reduce.10
  392.2 24.5 all-reduce.12
where the time goes:
time: 578 us; the launch traced here: 569 us
  blocking collectives  270 us (47%)
  waiting for transfers between devices  78.8 us (14%)
  matrix products  60.1 us (10%)
  starting transfers between devices  56.3 us (10%)
  other arithmetic  47.7 us (8%)
  local copies, waits for them, and re-layouts  39 us (7%)
  between operations  16.4 us (3%)
    all_to_all x9, waiting for transfers between devices, sent_and_summed(): lax.all_to_all(blocks, axis, split_axis=0, concat_axis=0, tiled=True)  56.3 us
    all_to_all x9, starting transfers between devices, sent_and_summed(): lax.all_to_all(blocks, axis, split_axis=0, concat_axis=0, tiled=True)  56.1 us
    all_gather x1, blocking collectives, body(): lax.all_gather(narrow_weight, 'dp', axis=1, tiled=True)  43.3 us
    all_gather x1, blocking collectives, body(): lax.all_gather(widen_weight, 'dp', axis=0, tiled=True)  42 us
    all_gather x1, blocking collectives, body(): lax.all_gather(qkv_weight, 'dp', axis=1, tiled=True)  39.6 us
    unnamed x1, blocking collectives  38.8 us
    all_gather x1, blocking collectives, body(): lax.all_gather(mix_weight, 'dp', axis=1, tiled=True)  38.7 us
    all_gather x1, blocking collectives, body(): lax.all_gather(qv_bias, 'dp', axis=2, tiled=True)  36.6 us
  transfers between devices with their start and end apart: 13, of which 7 were waited for; matrix products, arithmetic and copies ran while one was open for 12% of the time, Pallas kernels for 0%

commit v1 on v0

v1 whole, which is shorter than its diff:
```python
import functools

import jax
import jax.numpy as jnp
from jax import lax
from jax.experimental import pallas as pl
from jax.experimental.pallas import tpu as pltpu
from jax.sharding import PartitionSpec as P


HEAD_DIM = 64
EPS = 1e-06
BF = jnp.bfloat16
F32 = jnp.float32
AXES = ("dp", "mp")
GELU_A = 0.7978845608028654
GELU_B = 0.044715
BIAS = 64
LANES = 128
EXTRA = 16


def nn(a, b):
    return lax.dot_general(a, b, (((1,), (0,)), ((), ())), preferred_element_type=F32)


def nt(a, b):
    return lax.dot_general(a, b, (((1,), (1,)), ((), ())), preferred_element_type=F32)


def wide(column, tokens):
    return jnp.concatenate([column] * (tokens // LANES), axis=1)


def column_of(row):
    return jnp.broadcast_to(row, (LANES, row.shape[1])).T


def flipped(array):
    return array.astype(F32).T


def token_sum(array):
    return nt(jnp.ones((8, array.shape[1]), BF), array.astype(BF))


def normalized(x):
    mean = jnp.mean(x, axis=0, keepdims=True)
    centered = x - mean
    inverse = lax.rsqrt(jnp.mean(centered * centered, axis=0, keepdims=True) + EPS)
    return centered * inverse, inverse


def norm_back(grad, normed, inverse):
    first = jnp.mean(grad, axis=0, keepdims=True)
    second = jnp.mean(grad * normed, axis=0, keepdims=True)
    return (grad - first - normed * second) * inverse


def bit_orders(bits):
    down = list(range(bits - 1, -1, -1))
    other = down[:-2] + [down[-1], down[-2]] if bits > 1 else down
    return down, other


def place_of(apart, core, bits):
    orders = bit_orders(bits)
    places = [
        sum(((apart >> b) & 1) << p for p, b in enumerate(order)) for order in orders
    ]
    return jnp.where(core == 0, places[0], places[1])


def hop_pairs(phase, bits, dp, mp):
    orders = bit_orders(bits)
    return [
        (d * mp + c, (d ^ (1 << orders[c % 2][phase])) * mp + c)
        for d in range(dp)
        for c in range(mp)
    ]


def core_pairs(dp, mp):
    return [(d * mp + c, d * mp + (c ^ 1)) for d in range(dp) for c in range(mp)]


def pack_kernel(rows, adaln, adaln_b, qkv, qv_b, mix_t, mix_b, widen, widen_b, narrow_t,
                narrow_b, first_o, second_o, rows_s):
    core = lax.axis_index("mp")
    width = adaln.shape[1] // 6
    third, hidden = qkv.shape[2], widen.shape[1]
    half = rows // 2
    rows_s[...] = jnp.zeros_like(rows_s)
    rows_s[0:1, 0:half] = qv_b[0:1, :].astype(F32)
    rows_s[0:1, half:rows] = qv_b[1:2, :].astype(F32)
    rows_s[1:3, 0:rows] = adaln_b[0:2, :].astype(F32)
    rows_s[8:9, 0:rows] = widen_b[:, 0:rows].astype(F32)
    rows_s[9:10, 0:rows] = widen_b[:, rows : 2 * rows].astype(F32)
    rows_s[10:14, 0:rows] = adaln_b[2:6, :].astype(F32)
    rows_s[14:15, 0:rows] = mix_b[...].astype(F32)
    rows_s[15:16, 0:rows] = narrow_b[...].astype(F32)
    for out, at in ((first_o, 0), (second_o, 8)):
        turned = jnp.concatenate(
            [rows_s[at : at + 8, :], jnp.zeros((LANES - 8, LANES), F32)], axis=0).T
        out[:, out.shape[1] - BIAS :] = turned[0:rows, 0:BIAS].astype(BF)
    at = pl.multiple_of(core * width, LANES)
    first_o[:, 0:width] = adaln[:, pl.ds(at, width)]
    for j in range(3):
        first_o[:, width + j * third : width + (j + 1) * third] = qkv[j]
    at = pl.multiple_of((2 + 2 * core) * width, LANES)
    second_o[:, 0 : 2 * width] = adaln[:, pl.ds(at, 2 * width)]
    start = 2 * width
    second_o[:, start : start + hidden] = widen[...]
    second_o[:, start + hidden : start + 2 * hidden] = narrow_t[...]
    start += 2 * hidden
    second_o[:, start : start + third] = mix_t[...]


def gathered_blocks(where, dp, bits, mine, other):
    me, core = where[0], where[1]
    for parts, half in ((mine, core), (other, 1 - core)):
        for j in range(dp):
            at = place_of(me ^ j, half, bits)
            yield half, j, parts, at


def from_parts(parts, at, cut):
    low, high = parts
    count = low.shape[0]
    inside = lax.rem(at, count)
    return jnp.where(at < count, low[inside, :, cut], high[inside, :, cut])


def lane_only(block, lanes):
    keep = lax.broadcasted_iota(jnp.int32, block.shape, 1)
    return jnp.where(sum((keep == n).astype(jnp.int32) for n in lanes) > 0, block, 0.0)


def attention_kernel(dp, bits, rows, where, tok, cond, low, high, other_low, other_high,
                     att_o, qkv_o, prob_o, qkv_w_o, ada_o, mod_o,
                     qkv_t, bias_s, plain_s):
    step = pl.program_id(0)
    core = where[1]
    seq, width = tok.shape
    third = qkv_o.shape[1] // 3
    heads = third // HEAD_DIM
    ones = jnp.ones((EXTRA, seq), BF)

    @pl.when(step == 0)
    def _():
        plain_s[...] = jnp.zeros_like(plain_s)
        for half, j, parts, at in gathered_blocks(
                where, dp, bits, (low, high), (other_low, other_high)):
            keep = slice(j * rows, (j + 1) * rows)
            ada_o[half, keep, :] = from_parts(parts, at, slice(0, width))
            qkv_w_o[half, keep, :] = from_parts(parts, at, slice(width, width + 3 * third))
            bias = from_parts(parts, at, slice(width + 3 * third, width + 3 * third + BIAS))
            bias = bias.astype(F32)
            bias_s[keep, 0:BIAS] = bias
            column = lane_only(bias, (0,))
            n = rows // 2
            plain_s[half, j * n : (j + 1) * n, 0:BIAS] = column[0:n]
            plain_s[half, 2 * third + j * n : 2 * third + (j + 1) * n, 0:BIAS] = column[n:]
        bias_rows = bias_s[...].T
        act = cond[...].astype(F32)
        act = (act * jax.nn.sigmoid(act)).astype(BF)
        for h in range(2):
            qkv_t[h, :, 0:width] = flipped(qkv_w_o[h]).astype(BF)
            qkv_t[h, :, width:] = plain_s[h].astype(BF)
            mod_o[h] = nn(act, ada_o[h]) + bias_rows[1 + h : 2 + h, :]

    row = core * pl.num_programs(0) + step
    shift = column_of(mod_o[0, pl.ds(row, 1), :])
    lift = 1.0 + column_of(mod_o[1, pl.ds(row, 1), :])
    normed, _ = normalized(flipped(tok[...]))
    h1 = (normed * wide(lift, seq) + wide(shift, seq)).astype(BF)
    h1 = jnp.concatenate([h1, ones], axis=0)
    for h in range(2):
        qkv_o[h] = nn(qkv_t[h, :, 0 : width + EXTRA], h1).astype(BF)

    def scores_of(n):
        h, base = divmod(n, heads)
        base *= HEAD_DIM
        q = qkv_o[h, base : base + HEAD_DIM, :]
        k = qkv_o[h, third + base : third + base + HEAD_DIM, :]
        keys = flipped(k).astype(BF)
        return nn(keys, (q.astype(F32) * HEAD_DIM**-0.5).astype(BF))

    def finish(n, scores):
        h, base = divmod(n, heads)
        base *= HEAD_DIM
        v = qkv_o[h, 2 * third + base : 2 * third + base + HEAD_DIM, :]
        top = jnp.max(scores, axis=0, keepdims=True)
        raised = jnp.exp(scores - top)
        prob = (raised * (1.0 / jnp.sum(raised, axis=0, keepdims=True))).astype(BF)
        prob_o[n] = prob
        att_o[h, base : base + HEAD_DIM, :] = nn(v, prob).astype(BF)

    held = scores_of(0)
    for n in range(2 * heads):
        ahead = scores_of(n + 1) if n + 1 < 2 * heads else None
        finish(n, held)
        held = ahead


def put_blocks(dp, bits, where, outs, make):
    me, core = where[0], where[1]
    for out, half in zip(outs, (core, 1 - core)):
        for j in range(dp):
            out[place_of(me ^ j, half, bits)] = make(half, j).astype(BF)


def mlp_kernel(dp, bits, rows, where, tok, cot, att, cond, low, high, other_low, other_high,
               out_o, whole_o, datt_o, dx1_o, own_o, oth_o, own_d, oth_d, dact_o,
               widen_t, widen, narrow_t, narrow, mix_t, mix, ada, mods, bias_s, plain_s,
               w_acc, n_acc, m_acc, sums, dmods, g_s, du_s):
    step = pl.program_id(0)
    core = where[1]
    seq, width = cot.shape
    hidden = widen.shape[2]
    ones = jnp.ones((EXTRA, seq), BF)

    @pl.when(step == 0)
    def _():
        w_acc[...] = jnp.zeros_like(w_acc)
        n_acc[...] = jnp.zeros_like(n_acc)
        m_acc[...] = jnp.zeros_like(m_acc)
        sums[...] = jnp.zeros_like(sums)
        dmods[...] = jnp.zeros_like(dmods)
        plain_s[...] = jnp.zeros_like(plain_s)
        for half, j, parts, at in gathered_blocks(
                where, dp, bits, (low, high), (other_low, other_high)):
            keep = slice(j * rows, (j + 1) * rows)
            start = 0
            for ref in (ada, widen, narrow_t, mix_t):
                n = ref.shape[2]
                ref[half, keep, :] = from_parts(parts, at, slice(start, start + n))
                start += n
            bias = from_parts(parts, at, slice(start, start + BIAS)).astype(F32)
            bias_s[keep, 0:BIAS] = bias
            at = 2 * rows * j
            plain_s[half, at : at + rows, 0:BIAS] = lane_only(bias, (0,))
            plain_s[half, at + rows : at + 2 * rows, 0:BIAS] = lane_only(bias, (1,))
        bias_rows = bias_s[...].T
        act = cond[...].astype(F32)
        act = (act * jax.nn.sigmoid(act)).astype(BF)
        for h in range(2):
            widen_t[h, :, 0:width] = flipped(widen[h]).astype(BF)
            widen_t[h, :, width:] = plain_s[h].astype(BF)
            narrow[h] = flipped(narrow_t[h]).astype(BF)
            mix[h] = flipped(mix_t[h]).astype(BF)
            found = nn(act, ada[h])
            for p in range(2):
                n = 2 * h + p
                mods[n] = found[:, p * width : (p + 1) * width] + bias_rows[2 + n : 3 + n, :]

    row = core * pl.num_programs(0) + step
    gate1, shift2, scale2, gate2 = (
        wide(column_of(mods[n, pl.ds(row, 1), :]), seq) for n in range(4))
    abr = nn(mix_t[0], att[0]) + nn(mix_t[1], att[1])
    abr = abr + jnp.broadcast_to(bias_s[:, 6:7], abr.shape)
    x1 = flipped(tok[...]) + gate1 * abr
    normed, inverse = normalized(x1)
    lift = 1.0 + scale2
    h2 = (normed * lift + shift2).astype(BF)
    h2 = jnp.concatenate([h2, ones], axis=0)
    dy = flipped(cot[...])
    dm = (gate2 * dy).astype(BF)
    chunk = 256 if hidden % 256 == 0 else hidden
    cuts = [(h, slice(at, at + chunk)) for h in range(2) for at in range(0, hidden, chunk)]

    def grads(h, cut):
        n_acc[h, :, cut] += nt(dm, g_s[h, cut, :])
        w_acc[h, :, cut] += nt(h2[0 : width + 8], du_s[h, cut, :])

    def opened(h, cut):
        return nn(widen_t[h, cut, 0 : width + EXTRA], h2), nn(narrow[h, cut, :], dm)

    held = opened(*cuts[0])
    for n, (h, cut) in enumerate(cuts):
        u, dg = held
        if n + 1 < len(cuts):
            held = opened(*cuts[n + 1])
        if n > 0:
            grads(*cuts[n - 1])
        squared = u * u
        part = 0.5 * jnp.tanh(u * (GELU_A + (GELU_A * GELU_B) * squared)) + 0.5
        g = u * part
        slope = part + (g - g * part) * (2 * GELU_A + (6 * GELU_A * GELU_B) * squared)
        g_s[h, cut, :] = g.astype(BF)
        du_s[h, cut, :] = (dg * slope).astype(BF)
    grads(*cuts[-1])
    mbr = nn(narrow_t[0], g_s[0]) + nn(narrow_t[1], g_s[1])
    dh2 = nn(widen[0], du_s[0]) + nn(widen[1], du_s[1])
    mbr = mbr + jnp.broadcast_to(bias_s[:, 7:8], mbr.shape)
    y = (x1 + gate2 * mbr).T.astype(BF)
    out_o[...] = y
    whole_o[...] = y
    dx1 = dy + norm_back(dh2 * lift, normed, inverse)
    dx1_o[...] = dx1
    da = (gate1 * dx1).astype(BF)
    for h in range(2):
        m_acc[h] += nt(da, att[h])
        datt_o[h] = nn(mix[h], da).astype(BF)
    sums[0] += token_sum(da)
    sums[1] += token_sum(dm)
    for n, found in enumerate((dx1 * abr, dh2, dh2 * normed, dy * mbr)):
        dmods[n, pl.ds(row, 1), :] = token_sum(found)[0:1]

    @pl.when(step == pl.num_programs(0) - 1)
    def _():
        turned = [w_acc[h, width : width + 8, :].T for h in range(2)]
        flat = [sums[n].T for n in range(2)]
        for h in range(2):
            for j in range(dp):
                at = 2 * rows * j
                keep = slice(j * rows, (j + 1) * rows)
                cols = [flat[0][keep, 0:1], flat[1][keep, 0:1],
                        turned[h][at : at + rows, 0:1], turned[h][at + rows : at + 2 * rows, 0:1]]
                lane = lax.broadcasted_iota(jnp.int32, (rows, BIAS), 1)
                block = jnp.zeros((rows, BIAS), F32)
                for n, c in enumerate(cols):
                    block = jnp.where(lane == n, jnp.broadcast_to(c, block.shape), block)
                plain_s[h, keep, 0:BIAS] = block

        def make(half, j):
            keep = slice(j * rows, (j + 1) * rows)
            return jnp.concatenate(
                [w_acc[half, keep, :], n_acc[half, keep, :], m_acc[half, keep, :],
                 plain_s[half, keep, 0:BIAS]], axis=1)

        put_blocks(dp, bits, where, (own_o, oth_o), make)
        act = cond[...].astype(F32)
        act = act * jax.nn.sigmoid(act)
        mine = lax.broadcasted_iota(jnp.int32, act.shape, 0) // pl.num_programs(0) == core
        act = jnp.where(mine, act, 0.0).astype(BF)
        dact = jnp.zeros(act.shape, F32)
        for n in range(4):
            dact = dact + nt(dmods[n].astype(BF), ada[n // 2, :, (n % 2) * width : (n % 2 + 1) * width])
        dact_o[...] = dact
        for out, half in ((own_d, core), (oth_d, 1 - core)):
            for p in range(2):
                out[:, p * width : (p + 1) * width] = dmods[2 * half + p].astype(BF)
            out[:, 2 * width : 3 * width] = act


def back_kernel(dp, bits, rows, where, tok, cond, dx1_r, datt, qkv, prob_r, mods, qkv_w, ada,
                dact2, tok_o, whole_o, own_o, oth_o, rows_o, cond_o, q_acc, dmods, dqkv, plain_s):
    step = pl.program_id(0)
    core = where[1]
    seq, width = tok.shape
    third = qkv.shape[1] // 3
    heads = third // HEAD_DIM
    ones = jnp.ones((8, seq), BF)

    @pl.when(step == 0)
    def _():
        q_acc[...] = jnp.zeros_like(q_acc)
        dmods[...] = jnp.zeros_like(dmods)

    row = core * pl.num_programs(0) + step
    shift = wide(column_of(mods[0, pl.ds(row, 1), :]), seq)
    lift = 1.0 + wide(column_of(mods[1, pl.ds(row, 1), :]), seq)

    def dprob_of(n):
        h, base = divmod(n, heads)
        base *= HEAD_DIM
        v = qkv[h, 2 * third + base : 2 * third + base + HEAD_DIM, :]
        return nn(flipped(v).astype(BF), datt[h, base : base + HEAD_DIM, :])

    def finish(n, dprob):
        h, base = divmod(n, heads)
        base *= HEAD_DIM
        q = qkv[h, base : base + HEAD_DIM, :]
        k = qkv[h, third + base : third + base + HEAD_DIM, :]
        prob = prob_r[n]
        prob_f = prob.astype(F32)
        weighted = prob_f * dprob
        inner = jnp.sum(weighted, axis=0, keepdims=True)
        dscores = (weighted - prob_f * inner).astype(BF)
        dqkv[h, base : base + HEAD_DIM, :] = (nn(k, dscores) * HEAD_DIM**-0.5).astype(BF)
        dqkv[h, third + base : third + base + HEAD_DIM, :] = (
            nt(q, dscores) * HEAD_DIM**-0.5).astype(BF)
        dqkv[h, 2 * third + base : 2 * third + base + HEAD_DIM, :] = nt(
            datt[h, base : base + HEAD_DIM, :], prob).astype(BF)

    held = dprob_of(0)
    for n in range(2 * heads):
        ahead = dprob_of(n + 1) if n + 1 < 2 * heads else None
        finish(n, held)
        held = ahead
    normed, inverse = normalized(flipped(tok[...]))
    h1 = (normed * lift + shift).astype(BF)
    h1 = jnp.concatenate([h1, ones], axis=0)
    for h in range(2):
        q_acc[h] += nt(h1, dqkv[h])
    dh1 = nn(qkv_w[0], dqkv[0]) + nn(qkv_w[1], dqkv[1])
    grad = dx1_r[...] + norm_back(dh1 * lift, normed, inverse)
    grad = grad.T.astype(BF)
    tok_o[...] = grad
    whole_o[...] = grad
    for n, found in enumerate((dh1, dh1 * normed)):
        dmods[n, pl.ds(row, 1), :] = token_sum(found)[0:1]

    @pl.when(step == pl.num_programs(0) - 1)
    def _():
        n = rows // 2
        for h in range(2):
            turned = q_acc[h, width : width + 8, :].T
            for j in range(dp):
                for at, start in ((0, 0), (n, 2 * third)):
                    plain_s[h, j * rows + at : j * rows + at + n, :] = jnp.broadcast_to(
                        turned[start + j * n : start + (j + 1) * n, 0:1], (n, LANES))

        def make(half, j):
            keep = slice(j * rows, (j + 1) * rows)
            return jnp.concatenate(
                [q_acc[half, keep, :], plain_s[half, keep, 0:BIAS],
                 jnp.zeros((rows, own_o.shape[2] - 3 * third - BIAS), F32)], axis=1)

        put_blocks(dp, bits, where, (own_o, oth_o), make)
        c = cond[...].astype(F32)
        s = jax.nn.sigmoid(c)
        dact = dact2[...]
        for p in range(2):
            dact = dact + nt(dmods[p].astype(BF), ada[p])
        cond_o[...] = (dact * (s + c * s * (1.0 - s))).astype(BF)
        for p in range(2):
            rows_o[:, p * width : (p + 1) * width] = dmods[p].astype(BF)


def owned(me, rows, width):
    feature = lax.broadcasted_iota(jnp.int32, (width, LANES), 0)
    lane = lax.broadcasted_iota(jnp.int32, (width, LANES), 1)
    hit = jnp.where(lane < rows, (feature == rows * me + lane).astype(jnp.int32), 0)
    return hit.astype(F32).astype(BF)


def last_mlp_kernel(rows, width, where, kept, came, widen_o, narrow_o, mix_o, mix_b, narrow_b, widen_b,
                    ada_o, ada_b, act_o):
    hidden, third = widen_o.shape[1], mix_o.shape[1]
    total = kept[0:rows, :].astype(F32) + came[0:rows, :].astype(F32)
    widen_o[...] = total[:, 0:hidden]
    narrow_o[...] = total[:, hidden : 2 * hidden]
    mix_o[...] = total[:, 2 * hidden : 2 * hidden + third]
    small = total[:, 2 * hidden + third :].T
    mix_b[...] = small[0:1, :]
    narrow_b[...] = small[1:2, :]
    widen_b[:, 0:rows] = small[2:3, :]
    widen_b[:, rows : 2 * rows] = small[3:4, :]
    every = jnp.concatenate([kept[2 * rows :, 0 : 3 * width], came[rows:, 0 : 3 * width]], axis=0)
    pick = owned(where[0], rows, width)
    act = nn(every[:, 2 * width :], pick).T.astype(BF)
    act_o[...] = act
    ada_o[...] = nn(act, every[:, 0 : 2 * width])[0:rows]
    ada_b[...] = jnp.zeros_like(ada_b)
    for p in range(2):
        found = nn(every[:, p * width : (p + 1) * width], pick)
        ada_b[p : p + 1, :] = jnp.sum(found, axis=0, keepdims=True)


def last_back_kernel(rows, width, where, kept, came, act, early, early_other, early_b,
                     early_other_b, qkv_o, qv_b, ada_o, ada_b):
    third = qkv_o.shape[2]
    core = where[1]
    total = kept[0:rows, :].astype(F32) + came[0:rows, :].astype(F32)
    for j in range(3):
        qkv_o[j] = total[:, j * third : (j + 1) * third]
    small = total[:, 3 * third : 3 * third + BIAS].T
    n = rows // 2
    qv_b[0:1, :] = small[0:1, 0:n]
    qv_b[1:2, :] = small[0:1, n:rows]
    every = jnp.concatenate([kept[2 * rows :, :], came[rows:, :]], axis=0)
    ada_o[:, 0 : 2 * width] = nn(act[...], every)[0:rows]
    pick = owned(where[0], rows, width)
    for p in range(2):
        found = nn(every[:, p * width : (p + 1) * width], pick)
        ada_b[p : p + 1, :] = jnp.sum(found, axis=0, keepdims=True)[:, 0:rows]
    for half, values in ((core, early), (1 - core, early_other)):
        at = pl.multiple_of((2 + 2 * half) * width, LANES)
        ada_o[:, pl.ds(at, 2 * width)] = values[...]
    first = jnp.where(core == 0, early_b[...], early_other_b[...])
    second = jnp.where(core == 0, early_other_b[...], early_b[...])
    ada_b[2:4, :] = first[0:2, 0:rows]
    ada_b[4:6, :] = second[0:2, 0:rows]


def full(shape):
    return pl.BlockSpec(tuple(shape), lambda *_: (0,) * len(shape))


def cost(flops, nbytes):
    return pl.CostEstimate(flops=int(flops), bytes_accessed=int(nbytes), transcendentals=0)


PARAMS = pltpu.CompilerParams(vmem_limit_bytes=58 * 1024 * 1024)


def local_call(kernel, where, args, in_specs, outs, out_specs, scratch=(), grid=(1,), price=(1e6, 4e6)):
    return pl.pallas_call(
        kernel,
        out_shape=[jax.ShapeDtypeStruct(tuple(s), d) for s, d in outs],
        grid_spec=pltpu.PrefetchScalarGridSpec(
            num_scalar_prefetch=1, grid=grid, in_specs=in_specs, out_specs=out_specs,
            scratch_shapes=list(scratch)),
        compiler_params=PARAMS,
        cost_estimate=cost(*price),
    )(where, *args)


def plain_call(kernel, args, outs, scratch=()):
    return pl.pallas_call(
        kernel,
        out_shape=[jax.ShapeDtypeStruct(tuple(s), d) for s, d in outs],
        in_specs=[pl.BlockSpec(memory_space=pltpu.VMEM)] * len(args),
        out_specs=[pl.BlockSpec(memory_space=pltpu.VMEM)] * len(outs),
        scratch_shapes=list(scratch),
        compiler_params=PARAMS,
        cost_estimate=cost(1e6, 1e6),
    )(*args)


def whole_call(kernel, where, args, outs, scratch=()):
    return local_call(kernel, where, args, [full(a.shape) for a in args], outs,
                      [full(s) for s, _ in outs], scratch)


def hop(array, pairs):
    return lax.ppermute(array, AXES, pairs)


def gathered(message, bits, dp, mp):
    held = message[None]
    came = None
    for phase in range(bits):
        if came is not None:
            held = jnp.concatenate([held, came], axis=0)
        came = hop(held, hop_pairs(phase, bits, dp, mp))
    pairs = core_pairs(dp, mp)
    return held, came, hop(held, pairs), hop(came, pairs)


def reduced(own, other, own_rows, other_rows, bits, dp, mp):
    rows, wide_by = own.shape[1:]
    pairs = core_pairs(dp, mp)
    got = hop(other, pairs)
    got_rows = hop(other_rows, pairs)
    blocks = (own.astype(F32) + got.astype(F32)).astype(BF).reshape(dp * rows, wide_by)
    extra = (own_rows.astype(F32) + got_rows.astype(F32)).astype(BF)
    if extra.shape[1] < wide_by:
        extra = jnp.pad(extra, ((0, 0), (0, wide_by - extra.shape[1])))
    held = jnp.concatenate([blocks, extra], axis=0)
    for phase in reversed(range(bits)):
        n = (1 << phase) * rows
        came = hop(held[n:], hop_pairs(phase, bits, dp, mp))
        if phase:
            added = (held[:n].astype(F32) + came[:n].astype(F32)).astype(BF)
            held = jnp.concatenate([added, held[2 * n :], came[n:]], axis=0)
    return held, came


def body(
    tokens,
    condition,
    adaln_weight,
    adaln_bias,
    qkv_weight,
    qv_bias,
    mix_weight,
    mix_bias,
    widen_weight,
    widen_bias,
    narrow_weight,
    narrow_bias,
    cotangent,
):
    dp, mp = lax.axis_size("dp"), lax.axis_size("mp")
    bits = dp.bit_length() - 1
    me, core = lax.axis_index("dp"), lax.axis_index("mp")
    latents = condition.shape[0]
    own = latents // mp
    seq = tokens.shape[0] // latents
    width = tokens.shape[1]
    rows = width // dp
    third = qkv_weight.shape[2]
    hidden = widen_weight.shape[1]
    where = jnp.stack([me, core]).astype(jnp.int32)
    T = own * seq
    heads = 2 * third // HEAD_DIM

    first_width = width + 3 * third + BIAS
    second_width = 2 * width + 2 * hidden + third + BIAS
    first, second = plain_call(
        functools.partial(pack_kernel, rows),
        [adaln_weight, adaln_bias, qkv_weight, qv_bias.reshape(2, rows // 2), mix_weight.T,
         mix_bias.reshape(1, rows), widen_weight, widen_bias, narrow_weight.T,
         narrow_bias.reshape(1, rows)],
        [((rows, first_width), BF), ((rows, second_width), BF)],
        [pltpu.VMEM((16, LANES), F32)])

    part_a = gathered(first, bits, dp, mp)
    part_b = gathered(second, bits, dp, mp)

    tok_spec = pl.BlockSpec((seq, width), lambda i, w: (w[1] * own + i, 0))
    col = pl.BlockSpec((width, seq), lambda i, w: (0, i))
    half_col = lambda n: pl.BlockSpec((2, n, seq), lambda i, w: (0, 0, i))
    prob_spec = pl.BlockSpec((heads, seq, seq), lambda i, w: (i, 0, 0))
    flat = pl.BlockSpec((seq, width), lambda i, w: (i, 0))

    def fulls(arrays):
        return [full(a.shape) for a in arrays]

    att, qkv_act, prob, qkv_w, ada1, mods1 = local_call(
        functools.partial(attention_kernel, dp, bits, rows), where,
        [tokens, condition, *part_a],
        [tok_spec, full(condition.shape), *fulls(part_a)],
        [((2, third, T), BF), ((2, 3 * third, T), BF), ((own * heads, seq, seq), BF),
         ((2, width, 3 * third), BF), ((2, width, width), BF), ((2, latents, width), F32)],
        [half_col(third), half_col(3 * third), prob_spec, full((2, width, 3 * third)),
         full((2, width, width)), full((2, latents, width))],
        [pltpu.VMEM((2, 3 * third, width + LANES), BF), pltpu.VMEM((width, LANES), F32),
         pltpu.VMEM((2, 3 * third, LANES), F32)],
        grid=(own,), price=(3e9, 2e7))

    send_width = 2 * hidden + third + BIAS
    out_half, out_whole, datt, dx1, own_m, oth_m, own_md, oth_md, dact2 = local_call(
        functools.partial(mlp_kernel, dp, bits, rows), where,
        [tokens, cotangent, att, condition, *part_b],
        [tok_spec, tok_spec, half_col(third), full(condition.shape), *fulls(part_b)],
        [((T, width), BF), (tokens.shape, BF), ((2, third, T), BF), ((width, T), F32),
         ((dp, rows, send_width), BF), ((dp, rows, send_width), BF),
         ((latents, 3 * width), BF), ((latents, 3 * width), BF), ((latents, width), F32)],
        [flat, tok_spec, half_col(third), col, full((dp, rows, send_width)),
         full((dp, rows, send_width)), full((latents, 3 * width)), full((latents, 3 * width)),
         full((latents, width))],
        [pltpu.VMEM((2, hidden, width + LANES), BF), pltpu.VMEM((2, width, hidden), BF),
         pltpu.VMEM((2, width, hidden), BF), pltpu.VMEM((2, hidden, width), BF),
         pltpu.VMEM((2, width, third), BF), pltpu.VMEM((2, third, width), BF),
         pltpu.VMEM((2, width, 2 * width), BF), pltpu.VMEM((4, latents, width), F32),
         pltpu.VMEM((width, LANES), F32), pltpu.VMEM((2, hidden, LANES), F32),
         pltpu.VMEM((2, width + 8, hidden), F32), pltpu.VMEM((2, width, hidden), F32),
         pltpu.VMEM((2, width, third), F32), pltpu.VMEM((2, 8, width), F32),
         pltpu.VMEM((4, latents, width), F32), pltpu.VMEM((2, hidden, seq), BF),
         pltpu.VMEM((2, hidden, seq), BF)],
        grid=(own,), price=(8e9, 2e7))

    back_width = 2 * width
    tok_half, tok_whole, own_q, oth_q, rows_q, cond_own = local_call(
        functools.partial(back_kernel, dp, bits, rows), where,
        [tokens, condition, dx1, datt, qkv_act, prob, mods1, qkv_w, ada1, dact2],
        [tok_spec, full(condition.shape), col, half_col(third), half_col(3 * third), prob_spec,
         full(mods1.shape), full(qkv_w.shape), full(ada1.shape), full(dact2.shape)],
        [((T, width), BF), (tokens.shape, BF), ((dp, rows, back_width), BF),
         ((dp, rows, back_width), BF), ((latents, 2 * width), BF), ((latents, width), BF)],
        [flat, tok_spec, full((dp, rows, back_width)), full((dp, rows, back_width)),
         full((latents, 2 * width)), full((latents, width))],
        [pltpu.VMEM((2, width + 8, 3 * third), F32), pltpu.VMEM((2, latents, width), F32),
         pltpu.VMEM((2, 3 * third, seq), BF), pltpu.VMEM((2, width, LANES), F32)],
        grid=(own,), price=(6e9, 2e7))

    pairs = core_pairs(dp, mp)
    kept_m, came_m = reduced(own_m, oth_m, own_md, oth_md, bits, dp, mp)
    kept_q, came_q = reduced(own_q, oth_q, rows_q, rows_q, bits, dp, mp)
    condition_grad = (
        cond_own.astype(F32) + lax.ppermute(cond_own, AXES, pairs).astype(F32)).astype(BF)

    (widen_grad, narrow_grad, mix_grad, mix_b, narrow_b, widen_b, ada_m, ada_mb, act) = whole_call(
        functools.partial(last_mlp_kernel, rows, width), where, [kept_m, came_m],
        [((rows, hidden), F32), ((rows, hidden), F32), ((rows, third), F32), ((1, rows), F32),
         ((1, rows), F32), ((1, 2 * rows), F32), ((rows, 2 * width), F32), ((8, LANES), F32),
         ((LANES, dp * latents), BF)])
    qkv_grad, qv_b, adaln_weight_grad, adaln_bias_grad = whole_call(
        functools.partial(last_back_kernel, rows, width), where,
        [kept_q, came_q, act, ada_m, lax.ppermute(ada_m, AXES, pairs), ada_mb,
         lax.ppermute(ada_mb, AXES, pairs)],
        [((3, rows, third), F32), ((2, rows // 2), F32), ((rows, 6 * width), F32),
         ((6, rows), F32)])

    def joined(half, whole):
        came = lax.ppermute(half, AXES, pairs)
        return lax.dynamic_update_slice_in_dim(whole, came, (1 - core) * T, axis=0)

    return (
        joined(out_half, out_whole),
        joined(tok_half, tok_whole),
        condition_grad,
        adaln_weight_grad,
        adaln_bias_grad,
        qkv_grad,
        qv_b.reshape(2, 1, rows // 2),
        mix_grad.T,
        mix_b.reshape(rows),
        widen_grad,
        widen_b,
        narrow_grad.T,
        narrow_b.reshape(rows),
    )


def solution(mesh):
    return jax.shard_map(
        body,
        mesh=mesh,
        in_specs=(
            P("dp", None),
            P("dp", None),
            P("dp", None),
            P(None, "dp"),
            P(None, "dp", "mp"),
            P(None, "mp", "dp"),
            P("mp", "dp"),
            P("dp"),
            P("dp", "mp"),
            P("mp", "dp"),
            P("mp", "dp"),
            P("dp"),
            P("dp", None),
        ),
        out_specs=(
            P("dp", None),
            P("dp", None),
            P("dp", None),
            P("dp", None),
            P(None, "dp"),
            P(None, "dp", "mp"),
            P(None, "mp", "dp"),
            P("mp", "dp"),
            P("dp"),
            P("dp", "mp"),
            P("mp", "dp"),
            P("mp", "dp"),
            P("dp"),
        ),
        check_vma=False,
    )
```

time: 578 us -> 175 us (0.30)
  the two profiles are of different devices: /device:TPU:12 before, /device:TPU:0 now
where the time goes in v1:
time: 175 us; the launch traced here: 174 us
  waiting for transfers between devices  72 us (41%)
  Pallas kernels  57 us (33%)
  starting transfers between devices  30.7 us (18%)
  other arithmetic  7.93 us (5%)
  local copies, waits for them, and re-layouts  5.5 us (3%)
    ppermute x24, waiting for transfers between devices, hop(): return lax.ppermute(array, AXES, pairs)  71.1 us
    pallas_call x5, Pallas kernels, local_call(): pl.pallas_call(kernel, out_shape=[jax.ShapeDtypeStruct(tuple(s), d) for s...  55.1 us
    ppermute x24, starting transfers between devices, hop(): return lax.ppermute(array, AXES, pairs)  29.7 us
    unnamed x46, local copies, waits for them, and re-layouts  4.31 us
  transfers between devices with their start and end apart: 29, of which 18 were waited for; matrix products, arithmetic and copies ran while one was open for 5% of the time, Pallas kernels for 17%

profile of v1, /device:TPU:0, one launch (start us, length us, event | category | flops | bytes accessed | tf_op | source)
XLA Modules:
  0.0 174.2 jit_solution(9664696487421097080)
XLA Ops:
  0.6 1.9 %shard_map.228 = (bf16[24,1024]{1,0:T(8,128)(2,1)}, bf16[24,2560]{1,0:T(8,128)(2,1)}) custom-call(bf16[24,2304]{1,0:T(8,128)(2,1)} %adaln.1, bf16[6,24]{1,0:T(8,128)(2,1)} %adaln_b.1, bf16[3,24,192]{2,1,0:T(8,128)(2,1)} %qkv.1, bf16[2,12]{1,0:T(2,128)(2,1)} %bitcast.36, bf16[24,192]{1,0:T(8,128)(2,1)} %bitcast.35, bf16[1,24]{1,0:T(2,128)(2,1)} %bitcast.37, ...), custom_call_target="tpu_custom_call" | custom-call | flops 1000000 | bytes 1000000 | tf_op jit(solution)/shard_map/pallas_call | solution.py:512
  2.5 4.1 %collective-permute-start.6 = (bf16[1,24,2560]{2,1,0:T(8,128)(2,1)}, bf16[1,24,2560]{2,1,0:T(8,128)(2,1)S(1)}, u32[]{:S(2)}, u32[]{:S(2)}) collective-permute-start(bf16[1,24,2560]{2,1,0:T(8,128)(2,1)} %bitcast.26), channel_id=1, source_target_pairs={{0,16},{1,17},{2,18},{3,19},{4,20},{5,21},{6,22},{7,23},{8,24},{9,... | collective-permute-start | bytes 368648 | tf_op jit(solution)/shard_map/ppermute | solution.py:529
  6.6 6.2 %collective-permute-done.6 = bf16[1,24,2560]{2,1,0:T(8,128)(2,1)S(1)} collective-permute-done((bf16[1,24,2560]{2,1,0:T(8,128)(2,1)}, bf16[1,24,2560]{2,1,0:T(8,128)(2,1)S(1)}, u32[]{:S(2)}, u32[]{:S(2)}) %collective-permute-start.6) | collective-permute-done | bytes 122912 | tf_op jit(solution)/shard_map/ppermute | solution.py:529
  14.6 6.4 %collective-permute-done.7 = bf16[2,24,2560]{2,1,0:T(8,128)(2,1)S(1)} collective-permute-done((bf16[2,24,2560]{2,1,0:T(8,128)(2,1)S(1)}, bf16[2,24,2560]{2,1,0:T(8,128)(2,1)S(1)}, u32[]{:S(2)}, u32[]{:S(2)}) %collective-permute-start.7) | collective-permute-done | bytes 245792 | tf_op jit(solution)/shard_map/ppermute | solution.py:529
  23.3 7.5 %collective-permute-done.8 = bf16[4,24,2560]{2,1,0:T(8,128)(2,1)S(1)} collective-permute-done((bf16[4,24,2560]{2,1,0:T(8,128)(2,1)S(1)}, bf16[4,24,2560]{2,1,0:T(8,128)(2,1)S(1)}, u32[]{:S(2)}, u32[]{:S(2)}) %collective-permute-start.8) | collective-permute-done | bytes 491552 | tf_op jit(solution)/shard_map/ppermute | solution.py:529
  32.2 3.3 %collective-permute-start = (bf16[1,24,1024]{2,1,0:T(8,128)(2,1)S(1)}, bf16[1,24,1024]{2,1,0:T(8,128)(2,1)S(1)}, u32[]{:S(2)}, u32[]{:S(2)}) collective-permute-start(bf16[1,24,1024]{2,1,0:T(8,128)(2,1)S(1)} %bitcast.30), channel_id=1, source_target_pairs={{0,16},{1,17},{2,18},{3,19},{4,20},{5,21},{6,22},{7,23},{8,24},{9,... | collective-permute-start | bytes 147464 | tf_op jit(solution)/shard_map/ppermute | solution.py:529
  35.5 2.1 %collective-permute-done = bf16[1,24,1024]{2,1,0:T(8,128)(2,1)S(1)} collective-permute-done((bf16[1,24,1024]{2,1,0:T(8,128)(2,1)S(1)}, bf16[1,24,1024]{2,1,0:T(8,128)(2,1)S(1)}, u32[]{:S(2)}, u32[]{:S(2)}) %collective-permute-start) | collective-permute-done | bytes 49184 | tf_op jit(solution)/shard_map/ppermute | solution.py:529
  37.6 1.8 %collective-permute-start.1 = (bf16[2,24,1024]{2,1,0:T(8,128)(2,1)S(1)}, bf16[2,24,1024]{2,1,0:T(8,128)(2,1)S(1)}, u32[]{:S(2)}, u32[]{:S(2)}) collective-permute-start(bf16[2,24,1024]{2,1,0:T(8,128)(2,1)S(1)} %pad_maximum_fusion.17), channel_id=1, source_target_pairs={{0,8},{1,9},{2,10},{3,11},{4,12},{5,13},{6,14},{7,15},{8,0},{9,1},... | collective-permute-start | bytes 294920 | tf_op jit(solution)/shard_map/ppermute | solution.py:529
  39.4 2.9 %collective-permute-done.1 = bf16[2,24,1024]{2,1,0:T(8,128)(2,1)S(1)} collective-permute-done((bf16[2,24,1024]{2,1,0:T(8,128)(2,1)S(1)}, bf16[2,24,1024]{2,1,0:T(8,128)(2,1)S(1)}, u32[]{:S(2)}, u32[]{:S(2)}) %collective-permute-start.1) | collective-permute-done | bytes 98336 | tf_op jit(solution)/shard_map/ppermute | solution.py:529
  44.0 4.0 %collective-permute-done.2 = bf16[4,24,1024]{2,1,0:T(8,128)(2,1)S(1)} collective-permute-done((bf16[4,24,1024]{2,1,0:T(8,128)(2,1)S(1)}, bf16[4,24,1024]{2,1,0:T(8,128)(2,1)S(1)}, u32[]{:S(2)}, u32[]{:S(2)}) %collective-permute-start.2) | collective-permute-done | bytes 196640 | tf_op jit(solution)/shard_map/ppermute | solution.py:529
  49.3 6.7 %collective-permute-done.3.high = bf16[8,24,1024]{2,1,0:T(8,128)(2,1)} collective-permute-done((bf16[8,24,1024]{2,1,0:T(8,128)(2,1)S(1)}, bf16[8,24,1024]{2,1,0:T(8,128)(2,1)}, u32[]{:S(2)}, u32[]{:S(2)}) %collective-permute-start.3) | collective-permute-done | bytes 393248 | tf_op jit(solution)/shard_map/ppermute | solution.py:529
  58.1 12.0 %shard_map.229 = (bf16[2,192,1024]{2,1,0:T(8,128)(2,1)}, bf16[2,576,1024]{2,1,0:T(8,128)(2,1)}, bf16[24,256,256]{2,1,0:T(8,128)(2,1)}, bf16[2,384,576]{2,1,0:T(8...) custom-call(s32[2]{0:T(128)} %pad_add_fusion.where, bf16[2048,384]{1,0:T(8,128)(2,1)} %tok.5, ...), custom_call_target="tpu_custom_call" | custom-call | flops 3000000000 | bytes 20000000 | tf_op jit(solution)/shard_map/pallas_call | solution.py:500
  71.1 23.4 %shard_map.230 = (bf16[1024,384]{1,0:T(8,128)(2,1)}, bf16[2048,384]{1,0:T(8,128)(2,1)}, bf16[2,192,1024]{2,1,0:T(8,128)(2,1)}, f32[384,1024]{1,0:T(8,128)}, bf16...) custom-call(s32[2]{0:T(128)} %pad_add_fusion.where, ...), custom_call_target="tpu_custom_call" | custom-call | flops 8000000000 | bytes 20000000 | tf_op jit(solution)/shard_map/pallas_call | solution.py:500
  94.7 14.1 %shard_map.231 = (bf16[1024,384]{1,0:T(8,128)(2,1)}, bf16[2048,384]{1,0:T(8,128)(2,1)}, bf16[16,24,768]{2,1,0:T(8,128)(2,1)}, bf16[16,24,768]{2,1,0:T(8,128)(2,1...) custom-call(s32[2]{0:T(128)} %pad_add_fusion.where, bf16[2048,384]{1,0:T(8,128)(2,1)} %tok.5, bf16[8,384]{1,0:T(8,128)(2,1)} %cond.5, ...), custom_call_target="tpu_custom_call" | custom-call | flops 6000000000 | bytes 20000000 | tf_op jit(solution)/shard_map/pallas_call | solution.py:500
  115.6 4.3 %collective-permute-done.17 = bf16[200,768]{1,0:T(8,128)(2,1)S(1)} collective-permute-done((bf16[200,768]{1,0:T(8,128)(2,1)S(1)}, bf16[200,768]{1,0:T(8,128)(2,1)S(1)}, u32[]{:S(2)}, u32[]{:S(2)}) %collective-permute-start.17) | collective-permute-done | bytes 307232 | tf_op jit(solution)/shard_map/ppermute | solution.py:529
  122.9 5.4 %collective-permute-done.18 = bf16[112,768]{1,0:T(8,128)(2,1)} collective-permute-done((bf16[112,768]{1,0:T(8,128)(2,1)}, bf16[112,768]{1,0:T(8,128)(2,1)}, u32[]{:S(2)}, u32[]{:S(2)}) %collective-permute-start.18) | collective-permute-done | bytes 172064 | tf_op jit(solution)/shard_map/ppermute | solution.py:529
  130.0 1.8 %collective-permute-start.19 = (bf16[80,768]{1,0:T(8,128)(2,1)S(1)}, bf16[80,768]{1,0:T(8,128)(2,1)S(1)}, u32[]{:S(2)}, u32[]{:S(2)}) collective-permute-start(bf16[80,768]{1,0:T(8,128)(2,1)S(1)} %pad_maximum_fusion.14), channel_id=1, source_target_pairs={{0,8},{1,9},{2,10},{3,11},{4,12},{5,13},{6,14},{7,15},{8,0},{9,1},... | collective-permute-start | bytes 368648 | tf_op jit(solution)/shard_map/ppermute | solution.py:529
  132.2 2.0 %collective-permute-start.24 = (bf16[112,1792]{1,0:T(8,128)(2,1)S(1)}, bf16[112,1792]{1,0:T(8,128)(2,1)S(1)}, u32[]{:S(2)}, u32[]{:S(2)}) collective-permute-start(bf16[112,1792]{1,0:T(8,128)(2,1)S(1)} %pad_maximum_fusion.3), channel_id=1, source_target_pairs={{0,4},{1,3},{2,6},{3,1},{4,0},{5,7},{6,2},{7,5},{8,12},{9,11},{10,... | collective-permute-start | bytes 1204232 | tf_op jit(solution)/shard_map/ppermute | solution.py:529
  135.0 5.1 %collective-permute-done.24 = bf16[112,1792]{1,0:T(8,128)(2,1)S(1)} collective-permute-done((bf16[112,1792]{1,0:T(8,128)(2,1)S(1)}, bf16[112,1792]{1,0:T(8,128)(2,1)S(1)}, u32[]{:S(2)}, u32[]{:S(2)}) %collective-permute-start.24) | collective-permute-done | bytes 401440 | tf_op jit(solution)/shard_map/ppermute | solution.py:529
  141.4 5.5 %collective-permute-done.25 = bf16[80,1792]{1,0:T(8,128)(2,1)S(1)} collective-permute-done((bf16[80,1792]{1,0:T(8,128)(2,1)S(1)}, bf16[80,1792]{1,0:T(8,128)(2,1)S(1)}, u32[]{:S(2)}, u32[]{:S(2)}) %collective-permute-start.25) | collective-permute-done | bytes 286752 | tf_op jit(solution)/shard_map/ppermute | solution.py:529
  147.1 5.0 %collective-permute-start.26 = (bf16[88,1792]{1,0:T(8,128)(2,1)S(1)}, bf16[88,1792]{1,0:T(8,128)(2,1)S(1)}, u32[]{:S(2)}, u32[]{:S(2)}) collective-permute-start(bf16[88,1792]{1,0:T(8,128)(2,1)S(1)} %slice.133), channel_id=1, source_target_pairs={{0,16},{1,17},{2,18},{3,19},{4,20},{5,21},{6,22},{7,23},{8,24},{9,... | collective-permute-start | bytes 946184 | tf_op jit(solution)/shard_map/ppermute | solution.py:529
  153.5 12.2 %collective-permute-done.26.came = bf16[88,1792]{1,0:T(8,128)(2,1)S(1)} collective-permute-done((bf16[88,1792]{1,0:T(8,128)(2,1)S(1)}, bf16[88,1792]{1,0:T(8,128)(2,1)S(1)}, u32[]{:S(2)}, u32[]{:S(2)}) %collective-permute-start.26) | collective-permute-done | bytes 315424 | tf_op jit(solution)/shard_map/ppermute | solution.py:529
  166.4 2.9 %shard_map.232 = (f32[24,768]{1,0:T(8,128)}, f32[24,768]{1,0:T(8,128)}, f32[24,192]{1,0:T(8,128)}, f32[1,24]{1,0:T(1,128)}, f32[1,24]{1,0:T(1,128)}, /*index=5*/...) custom-call(s32[2]{0:T(128)} %pad_add_fusion.where, bf16[112,1792]{1,0:T(8,128)(2,1)} %copy-done, ...), custom_call_target="tpu_custom_call" | custom-call | flops 1000000 | bytes 4000000 | tf_op jit(solution)/shard_map/pallas_call | solution.py:500
  171.5 2.7 %shard_map.233 = (f32[3,24,192]{2,1,0:T(8,128)}, f32[2,12]{1,0:T(2,128)}, f32[24,2304]{1,0:T(8,128)}, f32[6,24]{1,0:T(8,128)}) custom-call(s32[2]{0:T(128)} %pad_add_fusion.where, bf16[112,768]{1,0:T(8,128)(2,1)} %copy-done.4, bf16[88,768]{1,0:T(8,128)(2,1)} %copy-done.8, bf16[128,128]{1,0:T(8,128)(2,1)} %get-tuple-element.72.act, ...), custom_call_target="tpu_custom_call" | custom-call | flops 1000000 | bytes 4000000 | tf_op jit(solution)/shard_map/pallas_call | solution.py:500
  (123 shorter events, 29.9 us)
Async XLA Ops:
  2.5 10.3 %collective-permute-start.6 = (bf16[1,24,2560]{2,1,0:T(8,128)(2,1)}, bf16[1,24,2560]{2,1,0:T(8,128)(2,1)S(1)}, u32[]{:S(2)}, u32[]{:S(2)}) collective-permute-start(bf16[1,24,2560]{2,1,0:T(8,128)(2,1)} %bitcast.26), channel_id=1, source_target_pairs={{0,16},{1,17},{2,18},{3,19},{4,20},{5,21},{6,22},{7,23},{8,24},{9,... | collective-permute-start | bytes 368648 | tf_op jit(solution)/shard_map/ppermute | solution.py:529
  13.8 7.2 %collective-permute-start.7 = (bf16[2,24,2560]{2,1,0:T(8,128)(2,1)S(1)}, bf16[2,24,2560]{2,1,0:T(8,128)(2,1)S(1)}, u32[]{:S(2)}, u32[]{:S(2)}) collective-permute-start(bf16[2,24,2560]{2,1,0:T(8,128)(2,1)S(1)} %pad_maximum_fusion.10), channel_id=1, source_target_pairs={{0,8},{1,9},{2,10},{3,11},{4,12},{5,13},{6,14},{7,15},{8,0},{9,1},... | collective-permute-start | bytes 737288 | tf_op jit(solution)/shard_map/ppermute | solution.py:529
  21.9 8.9 %collective-permute-start.8 = (bf16[4,24,2560]{2,1,0:T(8,128)(2,1)S(1)}, bf16[4,24,2560]{2,1,0:T(8,128)(2,1)S(1)}, u32[]{:S(2)}, u32[]{:S(2)}) collective-permute-start(bf16[4,24,2560]{2,1,0:T(8,128)(2,1)S(1)} %pad_maximum_fusion.2), channel_id=1, source_target_pairs={{0,4},{1,3},{2,6},{3,1},{4,0},{5,7},{6,2},{7,5},{8,12},{9,11},{10,... | collective-permute-start | bytes 1474568 | tf_op jit(solution)/shard_map/ppermute | solution.py:529
  30.9 17.8 %collective-permute-start.9 = (bf16[8,24,2560]{2,1,0:T(8,128)(2,1)S(1)}, bf16[8,24,2560]{2,1,0:T(8,128)(2,1)S(1)}, u32[]{:S(2)}, u32[]{:S(2)}) collective-permute-start(bf16[8,24,2560]{2,1,0:T(8,128)(2,1)S(1)} %pad_maximum_fusion.low), channel_id=1, source_target_pairs={{0,2},{1,5},{2,0},{3,7},{4,6},{5,1},{6,4},{7,3},{8,10},{9,13},{10,... | collective-permute-start | bytes 2949128 | tf_op jit(solution)/shard_map/ppermute | solution.py:529
  32.2 5.3 %collective-permute-start = (bf16[1,24,1024]{2,1,0:T(8,128)(2,1)S(1)}, bf16[1,24,1024]{2,1,0:T(8,128)(2,1)S(1)}, u32[]{:S(2)}, u32[]{:S(2)}) collective-permute-start(bf16[1,24,1024]{2,1,0:T(8,128)(2,1)S(1)} %bitcast.30), channel_id=1, source_target_pairs={{0,16},{1,17},{2,18},{3,19},{4,20},{5,21},{6,22},{7,23},{8,24},{9,... | collective-permute-start | bytes 147464 | tf_op jit(solution)/shard_map/ppermute | solution.py:529
  37.6 4.7 %collective-permute-start.1 = (bf16[2,24,1024]{2,1,0:T(8,128)(2,1)S(1)}, bf16[2,24,1024]{2,1,0:T(8,128)(2,1)S(1)}, u32[]{:S(2)}, u32[]{:S(2)}) collective-permute-start(bf16[2,24,1024]{2,1,0:T(8,128)(2,1)S(1)} %pad_maximum_fusion.17), channel_id=1, source_target_pairs={{0,8},{1,9},{2,10},{3,11},{4,12},{5,13},{6,14},{7,15},{8,0},{9,1},... | collective-permute-start | bytes 294920 | tf_op jit(solution)/shard_map/ppermute | solution.py:529
  42.3 5.7 %collective-permute-start.2 = (bf16[4,24,1024]{2,1,0:T(8,128)(2,1)S(1)}, bf16[4,24,1024]{2,1,0:T(8,128)(2,1)S(1)}, u32[]{:S(2)}, u32[]{:S(2)}) collective-permute-start(bf16[4,24,1024]{2,1,0:T(8,128)(2,1)S(1)} %pad_maximum_fusion.11), channel_id=1, source_target_pairs={{0,4},{1,3},{2,6},{3,1},{4,0},{5,7},{6,2},{7,5},{8,12},{9,11},{10,... | collective-permute-start | bytes 589832 | tf_op jit(solution)/shard_map/ppermute | solution.py:529
  48.1 7.9 %collective-permute-start.3 = (bf16[8,24,1024]{2,1,0:T(8,128)(2,1)S(1)}, bf16[8,24,1024]{2,1,0:T(8,128)(2,1)}, u32[]{:S(2)}, u32[]{:S(2)}) collective-permute-start(bf16[8,24,1024]{2,1,0:T(8,128)(2,1)S(1)} %pad_maximum_fusion.5.low), channel_id=1, source_target_pairs={{0,2},{1,5},{2,0},{3,7},{4,6},{5,1},{6,4},{7,3},{8,10},{9,13},{10,... | collective-permute-start | bytes 1179656 | tf_op jit(solution)/shard_map/ppermute | solution.py:529
  48.7 21.4 %collective-permute-start.10 = (bf16[8,24,2560]{2,1,0:T(8,128)(2,1)S(1)}, bf16[8,24,2560]{2,1,0:T(8,128)(2,1)S(1)}, u32[]{:S(2)}, u32[]{:S(2)}) collective-permute-start(bf16[8,24,2560]{2,1,0:T(8,128)(2,1)S(1)} %pad_maximum_fusion.low), channel_id=1, source_target_pairs={{0,1},{1,0},{2,3},{3,2},{4,5},{5,4},{6,7},{7,6},{8,9},{9,8},{10,11... | collective-permute-start | bytes 2949128 | tf_op jit(solution)/shard_map/ppermute | solution.py:529
  48.7 21.4 %collective-permute-start.11 = (bf16[8,24,2560]{2,1,0:T(8,128)(2,1)S(1)}, bf16[8,24,2560]{2,1,0:T(8,128)(2,1)}, u32[]{:S(2)}, u32[]{:S(2)}) collective-permute-start(bf16[8,24,2560]{2,1,0:T(8,128)(2,1)S(1)} %collective-permute-done.9.high), channel_id=1, source_target_pairs={{0,1},{1,0},{2,3},{3,2},{4,5},{5,4},{6,7},{7,6},{8,9},{9,8},{10,11... | collective-permute-start | bytes 2949128 | tf_op jit(solution)/shard_map/ppermute | solution.py:529
  49.2 7.5 %collective-permute-start.4 = (bf16[8,24,1024]{2,1,0:T(8,128)(2,1)S(1)}, bf16[8,24,1024]{2,1,0:T(8,128)(2,1)}, u32[]{:S(2)}, u32[]{:S(2)}) collective-permute-start(bf16[8,24,1024]{2,1,0:T(8,128)(2,1)S(1)} %pad_maximum_fusion.5.low), channel_id=1, source_target_pairs={{0,1},{1,0},{2,3},{3,2},{4,5},{5,4},{6,7},{7,6},{8,9},{9,8},{10,11... | collective-permute-start | bytes 1179656 | tf_op jit(solution)/shard_map/ppermute | solution.py:529
  94.5 19.1 %collective-permute-start.21 = (bf16[16,24,1792]{2,1,0:T(8,128)(2,1)}, bf16[16,24,1792]{2,1,0:T(8,128)(2,1)S(1)}, u32[]{:S(2)}, u32[]{:S(2)}) collective-permute-start(bf16[16,24,1792]{2,1,0:T(8,128)(2,1)} %get-tuple-element.69), channel_id=1, source_target_pairs={{0,1},{1,0},{2,3},{3,2},{4,5},{5,4},{6,7},{7,6},{8,9},{9,8},{10,11... | collective-permute-start | bytes 4128776 | tf_op jit(solution)/shard_map/ppermute | solution.py:529
  109.4 2.2 %collective-permute-start.15 = (bf16[16,24,768]{2,1,0:T(8,128)(2,1)}, bf16[16,24,768]{2,1,0:T(8,128)(2,1)S(1)}, u32[]{:S(2)}, u32[]{:S(2)}) collective-permute-start(bf16[16,24,768]{2,1,0:T(8,128)(2,1)} %get-tuple-element.66), channel_id=1, source_target_pairs={{0,1},{1,0},{2,3},{3,2},{4,5},{5,4},{6,7},{7,6},{8,9},{9,8},{10,11... | collective-permute-start | bytes 1769480 | tf_op jit(solution)/shard_map/ppermute | solution.py:529
  113.0 6.9 %collective-permute-start.17 = (bf16[200,768]{1,0:T(8,128)(2,1)S(1)}, bf16[200,768]{1,0:T(8,128)(2,1)S(1)}, u32[]{:S(2)}, u32[]{:S(2)}) collective-permute-start(bf16[200,768]{1,0:T(8,128)(2,1)S(1)} %pad_maximum_fusion.6), channel_id=1, source_target_pairs={{0,2},{1,5},{2,0},{3,7},{4,6},{5,1},{6,4},{7,3},{8,10},{9,13},{10,... | collective-permute-start | bytes 921608 | tf_op jit(solution)/shard_map/ppermute | solution.py:529
  114.1 17.8 %collective-permute-start.23 = (bf16[200,1792]{1,0:T(8,128)(2,1)S(1)}, bf16[200,1792]{1,0:T(8,128)(2,1)S(1)}, u32[]{:S(2)}, u32[]{:S(2)}) collective-permute-start(bf16[200,1792]{1,0:T(8,128)(2,1)S(1)} %pad_maximum_fusion.1), channel_id=1, source_target_pairs={{0,2},{1,5},{2,0},{3,7},{4,6},{5,1},{6,4},{7,3},{8,10},{9,13},{10,... | collective-permute-start | bytes 2150408 | tf_op jit(solution)/shard_map/ppermute | solution.py:529
  120.7 7.6 %collective-permute-start.18 = (bf16[112,768]{1,0:T(8,128)(2,1)}, bf16[112,768]{1,0:T(8,128)(2,1)}, u32[]{:S(2)}, u32[]{:S(2)}) collective-permute-start(bf16[112,768]{1,0:T(8,128)(2,1)} %pad_maximum_fusion.12), channel_id=1, source_target_pairs={{0,4},{1,3},{2,6},{3,1},{4,0},{5,7},{6,2},{7,5},{8,12},{9,11},{10,... | collective-permute-start | bytes 516104 | tf_op jit(solution)/shard_map/ppermute | solution.py:529
  122.4 11.8 %collective-permute-start.14 = (bf16[8,384]{1,0:T(8,128)(2,1)S(1)}, bf16[8,384]{1,0:T(8,128)(2,1)S(1)}, u32[]{:S(2)}, u32[]{:S(2)}) collective-permute-start(bf16[8,384]{1,0:T(8,128)(2,1)S(1)} %copy-done.11), channel_id=1, source_target_pairs={{0,1},{1,0},{2,3},{3,2},{4,5},{5,4},{6,7},{7,6},{8,9},{9,8},{10,11... | collective-permute-start | bytes 18440 | tf_op jit(solution)/shard_map/ppermute | solution.py:665
  122.4 29.8 %collective-permute-start.12 = (bf16[1024,384]{1,0:T(8,128)(2,1)}, bf16[1024,384]{1,0:T(8,128)(2,1)S(1)}, u32[]{:S(2)}, u32[]{:S(2)}) collective-permute-start(bf16[1024,384]{1,0:T(8,128)(2,1)} %get-tuple-element.53), channel_id=1, source_target_pairs={{0,1},{1,0},{2,3},{3,2},{4,5},{5,4},{6,7},{7,6},{8,9},{9,8},{10,11... | collective-permute-start | bytes 2359304 | tf_op jit(solution)/shard_map/ppermute | solution.py:680
  122.9 46.9 %collective-permute-start.13 = (bf16[1024,384]{1,0:T(8,128)(2,1)}, bf16[1024,384]{1,0:T(8,128)(2,1)S(1)}, u32[]{:S(2)}, u32[]{:S(2)}) collective-permute-start(bf16[1024,384]{1,0:T(8,128)(2,1)} %get-tuple-element.63), channel_id=1, source_target_pairs={{0,1},{1,0},{2,3},{3,2},{4,5},{5,4},{6,7},{7,6},{8,9},{9,8},{10,11... | collective-permute-start | bytes 2359304 | tf_op jit(solution)/shard_map/ppermute | solution.py:680
  130.0 4.9 %collective-permute-start.19 = (bf16[80,768]{1,0:T(8,128)(2,1)S(1)}, bf16[80,768]{1,0:T(8,128)(2,1)S(1)}, u32[]{:S(2)}, u32[]{:S(2)}) collective-permute-start(bf16[80,768]{1,0:T(8,128)(2,1)S(1)} %pad_maximum_fusion.14), channel_id=1, source_target_pairs={{0,8},{1,9},{2,10},{3,11},{4,12},{5,13},{6,14},{7,15},{8,0},{9,1},... | collective-permute-start | bytes 368648 | tf_op jit(solution)/shard_map/ppermute | solution.py:529
  132.2 7.9 %collective-permute-start.24 = (bf16[112,1792]{1,0:T(8,128)(2,1)S(1)}, bf16[112,1792]{1,0:T(8,128)(2,1)S(1)}, u32[]{:S(2)}, u32[]{:S(2)}) collective-permute-start(bf16[112,1792]{1,0:T(8,128)(2,1)S(1)} %pad_maximum_fusion.3), channel_id=1, source_target_pairs={{0,4},{1,3},{2,6},{3,1},{4,0},{5,7},{6,2},{7,5},{8,12},{9,11},{10,... | collective-permute-start | bytes 1204232 | tf_op jit(solution)/shard_map/ppermute | solution.py:529
  140.2 6.7 %collective-permute-start.25 = (bf16[80,1792]{1,0:T(8,128)(2,1)S(1)}, bf16[80,1792]{1,0:T(8,128)(2,1)S(1)}, u32[]{:S(2)}, u32[]{:S(2)}) collective-permute-start(bf16[80,1792]{1,0:T(8,128)(2,1)S(1)} %pad_maximum_fusion.7), channel_id=1, source_target_pairs={{0,8},{1,9},{2,10},{3,11},{4,12},{5,13},{6,14},{7,15},{8,0},{9,1},... | collective-permute-start | bytes 860168 | tf_op jit(solution)/shard_map/ppermute | solution.py:529
  147.1 18.6 %collective-permute-start.26 = (bf16[88,1792]{1,0:T(8,128)(2,1)S(1)}, bf16[88,1792]{1,0:T(8,128)(2,1)S(1)}, u32[]{:S(2)}, u32[]{:S(2)}) collective-permute-start(bf16[88,1792]{1,0:T(8,128)(2,1)S(1)} %slice.133), channel_id=1, source_target_pairs={{0,16},{1,17},{2,18},{3,19},{4,20},{5,21},{6,22},{7,23},{8,24},{9,... | collective-permute-start | bytes 946184 | tf_op jit(solution)/shard_map/ppermute | solution.py:529
  152.1 17.9 %collective-permute-start.20 = (bf16[88,768]{1,0:T(8,128)(2,1)S(1)}, bf16[88,768]{1,0:T(8,128)(2,1)S(1)}, u32[]{:S(2)}, u32[]{:S(2)}) collective-permute-start(bf16[88,768]{1,0:T(8,128)(2,1)S(1)} %slice.123), channel_id=1, source_target_pairs={{0,16},{1,17},{2,18},{3,19},{4,20},{5,21},{6,22},{7,23},{8,24},{9,... | collective-permute-start | bytes 405512 | tf_op jit(solution)/shard_map/ppermute | solution.py:529
  (25 other events, 247.4 us)

commit v2 on v1

--- a/solution.py
+++ b/solution.py
@@ -137,7 +137,7 @@
 
 
 def attention_kernel(dp, bits, rows, where, tok, cond, low, high, other_low, other_high,
-                     att_o, qkv_o, prob_o, qkv_w_o, ada_o, mod_o,
+                     att_o, qkv_o, prob_o, h1_o, qkv_w_o, ada_o, mod_o,
                      qkv_t, bias_s, plain_s):
     step = pl.program_id(0)
     core = where[1]
@@ -174,6 +174,7 @@
     lift = 1.0 + column_of(mod_o[1, pl.ds(row, 1), :])
     normed, _ = normalized(flipped(tok[...]))
     h1 = (normed * wide(lift, seq) + wide(shift, seq)).astype(BF)
+    h1_o[...] = h1
     h1 = jnp.concatenate([h1, ones], axis=0)
     for h in range(2):
         qkv_o[h] = nn(qkv_t[h, :, 0 : width + EXTRA], h1).astype(BF)
@@ -344,22 +345,14 @@
             out[:, 2 * width : 3 * width] = act
 
 
-def back_kernel(dp, bits, rows, where, tok, cond, dx1_r, datt, qkv, prob_r, mods, qkv_w, ada,
-                dact2, tok_o, whole_o, own_o, oth_o, rows_o, cond_o, q_acc, dmods, dqkv, plain_s):
+def back_kernel(start, own, where, tok, dx1_r, datt, qkv, prob_r, mods, qkv_w, *rest):
+    dqkv, sums_o, tok_o, whole_o = rest[-4:]
     step = pl.program_id(0)
     core = where[1]
-    seq, width = tok.shape
+    seq, _ = tok.shape
     third = qkv.shape[1] // 3
     heads = third // HEAD_DIM
-    ones = jnp.ones((8, seq), BF)
-
-    @pl.when(step == 0)
-    def _():
-        q_acc[...] = jnp.zeros_like(q_acc)
-        dmods[...] = jnp.zeros_like(dmods)
-
-    row = core * pl.num_programs(0) + step
-    shift = wide(column_of(mods[0, pl.ds(row, 1), :]), seq)
+    row = core * own + start + step
     lift = 1.0 + wide(column_of(mods[1, pl.ds(row, 1), :]), seq)
 
     def dprob_of(n):
@@ -390,92 +383,171 @@
         finish(n, held)
         held = ahead
     normed, inverse = normalized(flipped(tok[...]))
-    h1 = (normed * lift + shift).astype(BF)
-    h1 = jnp.concatenate([h1, ones], axis=0)
-    for h in range(2):
-        q_acc[h] += nt(h1, dqkv[h])
     dh1 = nn(qkv_w[0], dqkv[0]) + nn(qkv_w[1], dqkv[1])
     grad = dx1_r[...] + norm_back(dh1 * lift, normed, inverse)
     grad = grad.T.astype(BF)
     tok_o[...] = grad
     whole_o[...] = grad
     for n, found in enumerate((dh1, dh1 * normed)):
-        dmods[n, pl.ds(row, 1), :] = token_sum(found)[0:1]
-
-    @pl.when(step == pl.num_programs(0) - 1)
-    def _():
-        n = rows // 2
-        for h in range(2):
-            turned = q_acc[h, width : width + 8, :].T
-            for j in range(dp):
-                for at, start in ((0, 0), (n, 2 * third)):
-                    plain_s[h, j * rows + at : j * rows + at + n, :] = jnp.broadcast_to(
-                        turned[start + j * n : start + (j + 1) * n, 0:1], (n, LANES))
-
-        def make(half, j):
-            keep = slice(j * rows, (j + 1) * rows)
-            return jnp.concatenate(
-                [q_acc[half, keep, :], plain_s[half, keep, 0:BIAS],
-                 jnp.zeros((rows, own_o.shape[2] - 3 * third - BIAS), F32)], axis=1)
-
-        put_blocks(dp, bits, where, (own_o, oth_o), make)
-        c = cond[...].astype(F32)
-        s = jax.nn.sigmoid(c)
-        dact = dact2[...]
-        for p in range(2):
-            dact = dact + nt(dmods[p].astype(BF), ada[p])
-        cond_o[...] = (dact * (s + c * s * (1.0 - s))).astype(BF)
-        for p in range(2):
-            rows_o[:, p * width : (p + 1) * width] = dmods[p].astype(BF)
-
-
-def owned(me, rows, width):
+        sums_o[0, n] = token_sum(found)
+
+
+def grads_kernel(dp, bits, rows, own, calls, where, cond, h1, ada, dact2, *rest):
+    dqkv, sums = rest[:calls], rest[calls : 2 * calls]
+    own_o, oth_o, rows_o, cond_o, q_acc, dmods, plain_s = rest[2 * calls :]
+    core = where[1]
+    width = h1.shape[0]
+    third = dqkv[0].shape[1] // 3
+    every = h1.shape[1]
+    left = jnp.concatenate([h1[...], jnp.ones((8, every), BF)], axis=0)
+    n = rows // 2
+    for h in range(2):
+        right = jnp.concatenate([d[h] for d in dqkv], axis=1)
+        q_acc[h] = nt(left, right)
+        turned = q_acc[h, width : width + 8, :].T
+        for j in range(dp):
+            for at, start in ((0, 0), (n, 2 * third)):
+                plain_s[h, j * rows + at : j * rows + at + n, :] = jnp.broadcast_to(
+                    turned[start + j * n : start + (j + 1) * n, 0:1], (n, LANES))
+
+    def make(half, j):
+        keep = slice(j * rows, (j + 1) * rows)
+        return jnp.concatenate(
+            [q_acc[half, keep, :], plain_s[half, keep, 0:BIAS],
+             jnp.zeros((rows, own_o.shape[2] - 3 * third - BIAS), F32)], axis=1)
+
+    put_blocks(dp, bits, where, (own_o, oth_o), make)
+    dmods[...] = jnp.zeros_like(dmods)
+    at = 0
+    for part in sums:
+        for i in range(part.shape[0]):
+            for p in range(2):
+                dmods[p, pl.ds(core * own + at, 1), :] = part[i, p, 0:1, :]
+            at += 1
+    c = cond[...].astype(F32)
+    s = jax.nn.sigmoid(c)
+    dact = dact2[...]
+    for p in range(2):
+        dact = dact + nt(dmods[p].astype(BF), ada[p])
+    cond_o[...] = (dact * (s + c * s * (1.0 - s))).astype(BF)
+    for p in range(2):
+        rows_o[:, p * width : (p + 1) * width] = dmods[p].astype(BF)
+
+
+def apart_of(place, bits):
+    order = bit_orders(bits)[0]
+    return sum(((place >> p) & 1) << b for p, b in enumerate(order))
+
+
+def picked(me, rows, width, count, bits):
+    lane = lax.broadcasted_iota(jnp.int32, (1, LANES), 1)
+    wanted = jnp.full((1, LANES), -1, jnp.int32)
+    for k in range(count):
+        inside = lane - k * rows
+        target = rows * (me ^ apart_of(k, bits)) + inside
+        wanted = jnp.where(jnp.where(inside >= 0, inside, rows) < rows, target, wanted)
     feature = lax.broadcasted_iota(jnp.int32, (width, LANES), 0)
-    lane = lax.broadcasted_iota(jnp.int32, (width, LANES), 1)
-    hit = jnp.where(lane < rows, (feature == rows * me + lane).astype(jnp.int32), 0)
-    return hit.astype(F32).astype(BF)
-
-
-def last_mlp_kernel(rows, width, where, kept, came, widen_o, narrow_o, mix_o, mix_b, narrow_b, widen_b,
-                    ada_o, ada_b, act_o):
-    hidden, third = widen_o.shape[1], mix_o.shape[1]
-    total = kept[0:rows, :].astype(F32) + came[0:rows, :].astype(F32)
+    return (feature == jnp.broadcast_to(wanted, feature.shape)).astype(F32).astype(BF)
+
+
+def open_kernel(own, got, own_rows, got_rows, out):
+    count, rows = own.shape[0], own.shape[1]
+    half = count // 2
+    for k in range(half):
+        both = own[half + k].astype(F32) + got[half + k].astype(F32)
+        out[k * rows : (k + 1) * rows, :] = both.astype(BF)
+    both = (own_rows[...].astype(F32) + got_rows[...].astype(F32)).astype(BF)
+    n = own_rows.shape[0]
+    out[half * rows :, 0 : both.shape[1]] = both
+    if both.shape[1] < out.shape[1]:
+        out[half * rows :, both.shape[1] :] = jnp.zeros((n, out.shape[1] - both.shape[1]), BF)
+
+
+def second_kernel(own, got, sent, came, kept_o, out):
+    count, rows = own.shape[0], own.shape[1]
+    half, quarter = count // 2, count // 4
+    for k in range(half):
+        cut = slice(k * rows, (k + 1) * rows)
+        total = own[k].astype(F32) + got[k].astype(F32) + came[cut, :].astype(F32)
+        if k < quarter:
+            kept_o[cut, :] = total
+        else:
+            out[(k - quarter) * rows : (k - quarter + 1) * rows, :] = total.astype(BF)
+    n = came.shape[0] - half * rows
+    out[quarter * rows : quarter * rows + n, :] = sent[half * rows :, :]
+    out[quarter * rows + n :, :] = came[half * rows :, :]
+
+
+def middle_kernel(rows, width, bits, first_lane, pieces, used, *refs):
+    if pieces[1] is None:
+        kept, sent, came, act_in, kept_o, out = refs
+        me = lax.axis_index("dp")
+    else:
+        kept, sent, came, kept_o, out, act_in = refs
+        me = lax.axis_index("dp")
+    count = kept.shape[0]
+    near = count // 2
+    total = kept[...] + came[0:count, :].astype(F32)
+    every = jnp.concatenate([sent[count:, :], came[count:, :]], axis=0)
+    pick = picked(me, rows, width, count // rows, bits)
+    columns = pieces[0] * width
+    if pieces[1] is not None:
+        act = nn(every[:, pieces[1] * width : (pieces[1] + 1) * width], pick).T.astype(BF)
+        act_in[...] = act
+    else:
+        act = act_in[...]
+    ada = nn(act, every[:, 0:columns])[0:count]
+    lane = lax.broadcasted_iota(jnp.int32, (8, LANES), 0)
+    sums = jnp.zeros((8, LANES), F32)
+    for p in range(pieces[0]):
+        found = nn(every[:, p * width : (p + 1) * width], pick)
+        sums = jnp.where(lane == p, jnp.sum(found, axis=0, keepdims=True), sums)
+    turned = sums.T[0:count]
+    small = total[:, used - BIAS : used]
+    lane = lax.broadcasted_iota(jnp.int32, small.shape, 1)
+    for p in range(pieces[0]):
+        small = jnp.where(lane == first_lane + p, jnp.broadcast_to(turned[:, p : p + 1], small.shape), small)
+    joined = jnp.concatenate([total[:, 0 : used - BIAS], small, ada], axis=1)
+    kept_o[...] = joined[0:near]
+    out[...] = joined[near:].astype(BF)
+
+
+def step_kernel(kept, came, kept_o, out):
+    near = kept.shape[0] // 2
+    kept_o[...] = kept[0:near] + came[0:near, :].astype(F32)
+    out[...] = (kept[near:] + came[near:, :].astype(F32)).astype(BF)
+
+
+def last_mlp_kernel(rows, hidden, third, kept, came, widen_o, narrow_o, mix_o, mix_b, narrow_b,
+                    widen_b, ada_o, ada_b):
+    total = kept[...] + came[...].astype(F32)
     widen_o[...] = total[:, 0:hidden]
     narrow_o[...] = total[:, hidden : 2 * hidden]
     mix_o[...] = total[:, 2 * hidden : 2 * hidden + third]
-    small = total[:, 2 * hidden + third :].T
+    start = 2 * hidden + third
+    small = total[:, start : start + BIAS].T
     mix_b[...] = small[0:1, :]
     narrow_b[...] = small[1:2, :]
     widen_b[:, 0:rows] = small[2:3, :]
     widen_b[:, rows : 2 * rows] = small[3:4, :]
-    every = jnp.concatenate([kept[2 * rows :, 0 : 3 * width], came[rows:, 0 : 3 * width]], axis=0)
-    pick = owned(where[0], rows, width)
-    act = nn(every[:, 2 * width :], pick).T.astype(BF)
-    act_o[...] = act
-    ada_o[...] = nn(act, every[:, 0 : 2 * width])[0:rows]
+    ada_o[...] = total[:, start + BIAS :]
     ada_b[...] = jnp.zeros_like(ada_b)
-    for p in range(2):
-        found = nn(every[:, p * width : (p + 1) * width], pick)
-        ada_b[p : p + 1, :] = jnp.sum(found, axis=0, keepdims=True)
-
-
-def last_back_kernel(rows, width, where, kept, came, act, early, early_other, early_b,
-                     early_other_b, qkv_o, qv_b, ada_o, ada_b):
+    ada_b[0:2, 0:rows] = small[4:6, :]
+
+
+def last_back_kernel(rows, width, kept, came, early, early_other, early_b, early_other_b, qkv_o, qv_b,
+                     ada_o, ada_b):
     third = qkv_o.shape[2]
-    core = where[1]
-    total = kept[0:rows, :].astype(F32) + came[0:rows, :].astype(F32)
+    core = lax.axis_index("mp")
+    total = kept[...] + came[...].astype(F32)
     for j in range(3):
         qkv_o[j] = total[:, j * third : (j + 1) * third]
     small = total[:, 3 * third : 3 * third + BIAS].T
     n = rows // 2
     qv_b[0:1, :] = small[0:1, 0:n]
     qv_b[1:2, :] = small[0:1, n:rows]
-    every = jnp.concatenate([kept[2 * rows :, :], came[rows:, :]], axis=0)
-    ada_o[:, 0 : 2 * width] = nn(act[...], every)[0:rows]
-    pick = owned(where[0], rows, width)
-    for p in range(2):
-        found = nn(every[:, p * width : (p + 1) * width], pick)
-        ada_b[p : p + 1, :] = jnp.sum(found, axis=0, keepdims=True)[:, 0:rows]
+    ada_o[:, 0 : 2 * width] = total[:, 3 * third + BIAS :]
+    ada_b[0:2, :] = small[1:3, :]
     for half, values in ((core, early), (1 - core, early_other)):
         at = pl.multiple_of((2 + 2 * half) * width, LANES)
         ada_o[:, pl.ds(at, 2 * width)] = values[...]
@@ -493,70 +565,97 @@
     return pl.CostEstimate(flops=int(flops), bytes_accessed=int(nbytes), transcendentals=0)
 
 
-PARAMS = pltpu.CompilerParams(vmem_limit_bytes=58 * 1024 * 1024)
-
-
-def local_call(kernel, where, args, in_specs, outs, out_specs, scratch=(), grid=(1,), price=(1e6, 4e6)):
+MIB = {"pack": 58, "attention": 20, "mlp": 40, "back": 16}
+
+
+def params_of(name):
+    return pltpu.CompilerParams(vmem_limit_bytes=MIB.get(name.rstrip("0123456789"), 12) << 20)
+
+
+def local_call(kernel, where, args, in_specs, outs, out_specs, scratch=(), grid=(1,), price=(1e6, 4e6),
+               name=None, aliases=None):
     return pl.pallas_call(
         kernel,
         out_shape=[jax.ShapeDtypeStruct(tuple(s), d) for s, d in outs],
         grid_spec=pltpu.PrefetchScalarGridSpec(
             num_scalar_prefetch=1, grid=grid, in_specs=in_specs, out_specs=out_specs,
             scratch_shapes=list(scratch)),
-        compiler_params=PARAMS,
+        compiler_params=params_of(name),
         cost_estimate=cost(*price),
+        input_output_aliases=aliases or {},
     )(where, *args)
 
 
-def plain_call(kernel, args, outs, scratch=()):
+def plain_call(kernel, args, outs, scratch=(), name=None):
     return pl.pallas_call(
         kernel,
         out_shape=[jax.ShapeDtypeStruct(tuple(s), d) for s, d in outs],
         in_specs=[pl.BlockSpec(memory_space=pltpu.VMEM)] * len(args),
         out_specs=[pl.BlockSpec(memory_space=pltpu.VMEM)] * len(outs),
         scratch_shapes=list(scratch),
-        compiler_params=PARAMS,
+        compiler_params=params_of(name),
         cost_estimate=cost(1e6, 1e6),
     )(*args)
 
 
-def whole_call(kernel, where, args, outs, scratch=()):
+def whole_call(kernel, where, args, outs, scratch=(), name=None):
     return local_call(kernel, where, args, [full(a.shape) for a in args], outs,
-                      [full(s) for s, _ in outs], scratch)
+                      [full(s) for s, _ in outs], scratch, name=name)
 
 
 def hop(array, pairs):
     return lax.ppermute(array, AXES, pairs)
 
 
-def gathered(message, bits, dp, mp):
+def join_kernel(low, high, out):
+    n = low.shape[0]
+    out[0:n] = low[...]
+    out[n : 2 * n] = high[...]
+
+
+def gathered(message, bits, dp, mp, tag):
     held = message[None]
     came = None
     for phase in range(bits):
         if came is not None:
-            held = jnp.concatenate([held, came], axis=0)
+            shape = (2 * held.shape[0], *held.shape[1:])
+            held, = plain_call(join_kernel, [held, came], [(shape, BF)], name=f"{tag}join{phase}")
         came = hop(held, hop_pairs(phase, bits, dp, mp))
     pairs = core_pairs(dp, mp)
     return held, came, hop(held, pairs), hop(came, pairs)
 
 
-def reduced(own, other, own_rows, other_rows, bits, dp, mp):
+def reduced(own, other, own_rows, other_rows, bits, dp, mp, tag, width, used, first_lane, pieces, act=None):
     rows, wide_by = own.shape[1:]
     pairs = core_pairs(dp, mp)
     got = hop(other, pairs)
     got_rows = hop(other_rows, pairs)
-    blocks = (own.astype(F32) + got.astype(F32)).astype(BF).reshape(dp * rows, wide_by)
-    extra = (own_rows.astype(F32) + got_rows.astype(F32)).astype(BF)
-    if extra.shape[1] < wide_by:
-        extra = jnp.pad(extra, ((0, 0), (0, wide_by - extra.shape[1])))
-    held = jnp.concatenate([blocks, extra], axis=0)
-    for phase in reversed(range(bits)):
-        n = (1 << phase) * rows
-        came = hop(held[n:], hop_pairs(phase, bits, dp, mp))
+    extra = own_rows.shape[0]
+    n = dp // 2 * rows
+    sent, = plain_call(open_kernel, [own, got, own_rows, got_rows], [((n + extra, wide_by), BF)],
+                       name=f"{tag}open")
+    came = hop(sent, hop_pairs(bits - 1, bits, dp, mp))
+    n //= 2
+    kept, sent = plain_call(second_kernel, [own, got, sent, came],
+                            [((n, wide_by), F32), ((n + 2 * extra, wide_by), BF)], name=f"{tag}second")
+    came = hop(sent, hop_pairs(bits - 2, bits, dp, mp))
+    columns = used + pieces[0] * width
+    outs = [((n // 2, columns), F32), ((n // 2, columns), BF)]
+    ins = [kept, sent, came]
+    if act is None:
+        outs.append(((LANES, 4 * extra), BF))
+    else:
+        ins.append(act)
+    kept, sent, *acts = plain_call(
+        functools.partial(middle_kernel, rows, width, bits, first_lane, pieces, used), ins, outs,
+        name=f"{tag}middle")
+    for phase in reversed(range(bits - 2)):
+        came = hop(sent, hop_pairs(phase, bits, dp, mp))
         if phase:
-            added = (held[:n].astype(F32) + came[:n].astype(F32)).astype(BF)
-            held = jnp.concatenate([added, held[2 * n :], came[n:]], axis=0)
-    return held, came
+            n = kept.shape[0] // 2
+            kept, sent = plain_call(step_kernel, [kept, came], [((n, columns), F32), ((n, columns), BF)],
+                                    name=f"{tag}step{phase}")
+    return kept, came, acts
 
 
 def body(
@@ -596,10 +695,10 @@
          mix_bias.reshape(1, rows), widen_weight, widen_bias, narrow_weight.T,
          narrow_bias.reshape(1, rows)],
         [((rows, first_width), BF), ((rows, second_width), BF)],
-        [pltpu.VMEM((16, LANES), F32)])
-
-    part_a = gathered(first, bits, dp, mp)
-    part_b = gathered(second, bits, dp, mp)
+        [pltpu.VMEM((16, LANES), F32)], name="pack")
+
+    part_a = gathered(first, bits, dp, mp, "a")
+    part_b = gathered(second, bits, dp, mp, "b")
 
     tok_spec = pl.BlockSpec((seq, width), lambda i, w: (w[1] * own + i, 0))
     col = pl.BlockSpec((width, seq), lambda i, w: (0, i))
@@ -610,17 +709,17 @@
     def fulls(arrays):
         return [full(a.shape) for a in arrays]
 
-    att, qkv_act, prob, qkv_w, ada1, mods1 = local_call(
+    att, qkv_act, prob, h1, qkv_w, ada1, mods1 = local_call(
         functools.partial(attention_kernel, dp, bits, rows), where,
         [tokens, condition, *part_a],
         [tok_spec, full(condition.shape), *fulls(part_a)],
         [((2, third, T), BF), ((2, 3 * third, T), BF), ((own * heads, seq, seq), BF),
-         ((2, width, 3 * third), BF), ((2, width, width), BF), ((2, latents, width), F32)],
-        [half_col(third), half_col(3 * third), prob_spec, full((2, width, 3 * third)),
+         ((width, T), BF), ((2, width, 3 * third), BF), ((2, width, width), BF), ((2, latents, width), F32)],
+        [half_col(third), half_col(3 * third), prob_spec, col, full((2, width, 3 * third)),
          full((2, width, width)), full((2, latents, width))],
         [pltpu.VMEM((2, 3 * third, width + LANES), BF), pltpu.VMEM((width, LANES), F32),
          pltpu.VMEM((2, 3 * third, LANES), F32)],
-        grid=(own,), price=(3e9, 2e7))
+        grid=(own,), price=(3e9, 2e7), name="attention")
 
     send_width = 2 * hidden + third + BIAS
     out_half, out_whole, datt, dx1, own_m, oth_m, own_md, oth_md, dact2 = local_call(
@@ -642,47 +741,73 @@
          pltpu.VMEM((2, width, third), F32), pltpu.VMEM((2, 8, width), F32),
          pltpu.VMEM((4, latents, width), F32), pltpu.VMEM((2, hidden, seq), BF),
          pltpu.VMEM((2, hidden, seq), BF)],
-        grid=(own,), price=(8e9, 2e7))
+        grid=(own,), price=(8e9, 2e7), name="mlp")
 
     back_width = 2 * width
-    tok_half, tok_whole, own_q, oth_q, rows_q, cond_own = local_call(
-        functools.partial(back_kernel, dp, bits, rows), where,
-        [tokens, condition, dx1, datt, qkv_act, prob, mods1, qkv_w, ada1, dact2],
-        [tok_spec, full(condition.shape), col, half_col(third), half_col(3 * third), prob_spec,
-         full(mods1.shape), full(qkv_w.shape), full(ada1.shape), full(dact2.shape)],
-        [((T, width), BF), (tokens.shape, BF), ((dp, rows, back_width), BF),
-         ((dp, rows, back_width), BF), ((latents, 2 * width), BF), ((latents, width), BF)],
-        [flat, tok_spec, full((dp, rows, back_width)), full((dp, rows, back_width)),
-         full((latents, 2 * width)), full((latents, width))],
+    splits = [1, own - 1] if own > 1 else [own]
+    dqkv, sums, halves, whole, at = [], [], None, None, 0
+    for number, count in enumerate(splits):
+        first_at = at
+        tok_at = pl.BlockSpec((seq, width), lambda i, w, s=first_at: (w[1] * own + s + i, 0))
+        ins = [tokens, dx1, datt, qkv_act, prob, mods1, qkv_w]
+        in_specs = [
+            tok_at, pl.BlockSpec((width, seq), lambda i, w, s=first_at: (0, i + s)),
+            *(pl.BlockSpec((2, n, seq), lambda i, w, s=first_at: (0, 0, i + s))
+              for n in (third, 3 * third)),
+            pl.BlockSpec((heads, seq, seq), lambda i, w, s=first_at: (i + s, 0, 0)),
+            full(mods1.shape), full(qkv_w.shape)]
+        aliases = {}
+        if whole is not None:
+            aliases = {1 + len(ins): 2, 2 + len(ins): 3}
+            ins += [halves, whole]
+            in_specs += [pl.BlockSpec(memory_space=pl.ANY)] * 2
+        d, s_rows, halves, whole = local_call(
+            functools.partial(back_kernel, at, own), where, ins, in_specs,
+            [((2, 3 * third, count * seq), BF), ((count, 2, 8, width), F32),
+             ((T, width), BF), (tokens.shape, BF)],
+            [half_col(3 * third), pl.BlockSpec((1, 2, 8, width), lambda i, w: (i, 0, 0, 0)),
+             pl.BlockSpec((seq, width), lambda i, w, s=first_at: (i + s, 0)), tok_at],
+            grid=(count,), price=(1.5e9 * count, 5e6), name=f"back{number}", aliases=aliases)
+        dqkv.append(d)
+        sums.append(s_rows)
+        at += count
+    tok_whole = whole
+    own_q, oth_q, rows_q, cond_own = whole_call(
+        functools.partial(grads_kernel, dp, bits, rows, own, len(splits)), where,
+        [condition, h1, ada1, dact2, *dqkv, *sums],
+        [((dp, rows, back_width), BF), ((dp, rows, back_width), BF), ((latents, 2 * width), BF),
+         ((latents, width), BF)],
         [pltpu.VMEM((2, width + 8, 3 * third), F32), pltpu.VMEM((2, latents, width), F32),
-         pltpu.VMEM((2, 3 * third, seq), BF), pltpu.VMEM((2, width, LANES), F32)],
-        grid=(own,), price=(6e9, 2e7))
+         pltpu.VMEM((2, width, LANES), F32)], name="grads")
 
     pairs = core_pairs(dp, mp)
-    kept_m, came_m = reduced(own_m, oth_m, own_md, oth_md, bits, dp, mp)
-    kept_q, came_q = reduced(own_q, oth_q, rows_q, rows_q, bits, dp, mp)
+    kept_m, came_m, (act,) = reduced(
+        own_m, oth_m, own_md, oth_md, bits, dp, mp, "m", width, send_width, 4, (2, 2))
+    kept_q, came_q, _ = reduced(
+        own_q, oth_q, rows_q, rows_q, bits, dp, mp, "q", width, 3 * third + BIAS, 1, (2, None), act)
     condition_grad = (
         cond_own.astype(F32) + lax.ppermute(cond_own, AXES, pairs).astype(F32)).astype(BF)
 
-    (widen_grad, narrow_grad, mix_grad, mix_b, narrow_b, widen_b, ada_m, ada_mb, act) = whole_call(
-        functools.partial(last_mlp_kernel, rows, width), where, [kept_m, came_m],
+    (widen_grad, narrow_grad, mix_grad, mix_b, narrow_b, widen_b, ada_m, ada_mb) = plain_call(
+        functools.partial(last_mlp_kernel, rows, hidden, third), [kept_m, came_m],
         [((rows, hidden), F32), ((rows, hidden), F32), ((rows, third), F32), ((1, rows), F32),
-         ((1, rows), F32), ((1, 2 * rows), F32), ((rows, 2 * width), F32), ((8, LANES), F32),
-         ((LANES, dp * latents), BF)])
-    qkv_grad, qv_b, adaln_weight_grad, adaln_bias_grad = whole_call(
-        functools.partial(last_back_kernel, rows, width), where,
-        [kept_q, came_q, act, ada_m, lax.ppermute(ada_m, AXES, pairs), ada_mb,
+         ((1, rows), F32), ((1, 2 * rows), F32), ((rows, 2 * width), F32), ((8, LANES), F32)],
+        name="last_mlp")
+    qkv_grad, qv_b, adaln_weight_grad, adaln_bias_grad = plain_call(
+        functools.partial(last_back_kernel, rows, width),
+        [kept_q, came_q, ada_m, lax.ppermute(ada_m, AXES, pairs), ada_mb,
          lax.ppermute(ada_mb, AXES, pairs)],
         [((3, rows, third), F32), ((2, rows // 2), F32), ((rows, 6 * width), F32),
-         ((6, rows), F32)])
+         ((6, rows), F32)],
+        name="last_back")
 
     def joined(half, whole):
-        came = lax.ppermute(half, AXES, pairs)
+        came = hop(half, pairs)
         return lax.dynamic_update_slice_in_dim(whole, came, (1 - core) * T, axis=0)
 
     return (
         joined(out_half, out_whole),
-        joined(tok_half, tok_whole),
+        joined(halves, tok_whole),
         condition_grad,
         adaln_weight_grad,
         adaln_bias_grad,

time: 175 us -> 143 us (0.82)
  waiting for transfers between devices: 72 us -> 54.8 us
  other arithmetic: 7.93 us -> 0.67 us
  Pallas kernels: 57 us -> 52.4 us
  local copies, waits for them, and re-layouts: 5.5 us -> 3.19 us
    ppermute x24 -> x26, waiting for transfers between devices: 71.1 us -> 54.1 us  [hop(): return lax.ppermute(array, AXES, pairs)]
    pallas_call x5, Pallas kernels: 55.1 us -> 46.9 us  [local_call(): pl.pallas_call(kernel, out_shape=[jax.ShapeDtypeStruct(tuple(s), d) for s...]
    convert_element_type x8 -> x0, other arithmetic: 3.75 us -> none  [the longest x2 1.67 us: reduced(): (own.astype(F32) + got.astype(F32)).astype(BF).reshape(dp * rows, wide_by)]
    pallas_call x1 -> x17, Pallas kernels: 1.86 us -> 5.53 us  [plain_call(): pl.pallas_call(kernel, out_shape=[jax.ShapeDtypeStruct(tuple(s), d) for s...]
    unnamed x46 -> x14, local copies, waits for them, and re-layouts: 4.31 us -> 0.94 us
    concatenate x12 -> x0, other arithmetic: 2.87 us -> none  [the longest x6 2.05 us: gathered(): held = jnp.concatenate([held, came], axis=0)]
    dynamic_update_slice x2, local copies, waits for them, and re-layouts: 0.32 us -> 2.25 us  [joined(): return lax.dynamic_update_slice_in_dim(whole, came, (1 - core) * T, axis=0)]
    ppermute x24 -> x26, starting transfers between devices: 29.7 us -> 30.3 us  [hop(): return lax.ppermute(array, AXES, pairs)]
  transfers between devices with their start and end apart: 29 -> 29, of which waited for: 18 -> 16; matrix products, arithmetic and copies ran while one was open for 5% -> 2% of each run, Pallas kernels for 17% -> 19%
where the time goes in v2:
time: 143 us
  waiting for transfers between devices  54.8 us (38%)
  Pallas kernels  52.4 us (37%)
  starting transfers between devices  30.9 us (22%)
  local copies, waits for them, and re-layouts  3.19 us (2%)
    ppermute x26, waiting for transfers between devices, hop(): return lax.ppermute(array, AXES, pairs)  54.1 us
    pallas_call x5, Pallas kernels, local_call(): pl.pallas_call(kernel, out_shape=[jax.ShapeDtypeStruct(tuple(s), d) for s...  46.9 us
    ppermute x26, starting transfers between devices, hop(): return lax.ppermute(array, AXES, pairs)  30.3 us
    pallas_call x17, Pallas kernels, plain_call(): pl.pallas_call(kernel, out_shape=[jax.ShapeDtypeStruct(tuple(s), d) for s...  5.53 us
  transfers between devices with their start and end apart: 29, of which 16 were waited for; matrix products, arithmetic and copies ran while one was open for 2% of the time, Pallas kernels for 19%

profile of v2, /device:TPU:0, one launch (start us, length us, event | category | flops | bytes accessed | tf_op | source)
XLA Modules:
  0.0 142.8 jit_solution(11217700539986142975)
XLA Ops:
  0.6 1.9 %shard_map.228 = (bf16[24,1024]{1,0:T(8,128)(2,1)}, bf16[24,2560]{1,0:T(8,128)(2,1)}) custom-call(bf16[24,2304]{1,0:T(8,128)(2,1)} %adaln.1, bf16[6,24]{1,0:T(8,128)(2,1)} %adaln_b.1, bf16[3,24,192]{2,1,0:T(8,128)(2,1)} %qkv.1, bf16[2,12]{1,0:T(2,128)(2,1)} %bitcast.22, bf16[24,192]{1,0:T(8,128)(2,1)} %bitcast.21, bf16[1,24]{1,0:T(2,128)(2,1)} %bitcast.23, ...), custom_call_target="tpu_custom_call" | custom-call | flops 1000000 | bytes 1000000 | tf_op jit(solution)/shard_map/pallas_call | solution.py:590
  2.5 4.1 %collective-permute-start.6 = (bf16[1,24,2560]{2,1,0:T(8,128)(2,1)}, bf16[1,24,2560]{2,1,0:T(8,128)(2,1)S(1)}, u32[]{:S(2)}, u32[]{:S(2)}) collective-permute-start(bf16[1,24,2560]{2,1,0:T(8,128)(2,1)} %bitcast.16), channel_id=1, source_target_pairs={{0,16},{1,17},{2,18},{3,19},{4,20},{5,21},{6,22},{7,23},{8,24},{9,... | collective-permute-start | bytes 368648 | tf_op jit(solution)/shard_map/ppermute | solution.py:607
  6.6 6.2 %collective-permute-done.6.high = bf16[1,24,2560]{2,1,0:T(8,128)(2,1)S(1)} collective-permute-done((bf16[1,24,2560]{2,1,0:T(8,128)(2,1)}, bf16[1,24,2560]{2,1,0:T(8,128)(2,1)S(1)}, u32[]{:S(2)}, u32[]{:S(2)}) %collective-permute-start.6) | collective-permute-done | bytes 122912 | tf_op jit(solution)/shard_map/ppermute | solution.py:607
  14.6 6.3 %collective-permute-done.7.high = bf16[2,24,2560]{2,1,0:T(8,128)(2,1)S(1)} collective-permute-done((bf16[2,24,2560]{2,1,0:T(8,128)(2,1)S(1)}, bf16[2,24,2560]{2,1,0:T(8,128)(2,1)S(1)}, u32[]{:S(2)}, u32[]{:S(2)}) %collective-permute-start.7) | collective-permute-done | bytes 245792 | tf_op jit(solution)/shard_map/ppermute | solution.py:607
  22.4 7.5 %collective-permute-done.8.high = bf16[4,24,2560]{2,1,0:T(8,128)(2,1)S(1)} collective-permute-done((bf16[4,24,2560]{2,1,0:T(8,128)(2,1)S(1)}, bf16[4,24,2560]{2,1,0:T(8,128)(2,1)S(1)}, u32[]{:S(2)}, u32[]{:S(2)}) %collective-permute-start.8) | collective-permute-done | bytes 491552 | tf_op jit(solution)/shard_map/ppermute | solution.py:607
  31.3 3.3 %collective-permute-start = (bf16[1,24,1024]{2,1,0:T(8,128)(2,1)S(1)}, bf16[1,24,1024]{2,1,0:T(8,128)(2,1)S(1)}, u32[]{:S(2)}, u32[]{:S(2)}) collective-permute-start(bf16[1,24,1024]{2,1,0:T(8,128)(2,1)S(1)} %bitcast.18), channel_id=1, source_target_pairs={{0,16},{1,17},{2,18},{3,19},{4,20},{5,21},{6,22},{7,23},{8,24},{9,... | collective-permute-start | bytes 147464 | tf_op jit(solution)/shard_map/ppermute | solution.py:607
  34.6 2.1 %collective-permute-done.high = bf16[1,24,1024]{2,1,0:T(8,128)(2,1)S(1)} collective-permute-done((bf16[1,24,1024]{2,1,0:T(8,128)(2,1)S(1)}, bf16[1,24,1024]{2,1,0:T(8,128)(2,1)S(1)}, u32[]{:S(2)}, u32[]{:S(2)}) %collective-permute-start) | collective-permute-done | bytes 49184 | tf_op jit(solution)/shard_map/ppermute | solution.py:607
  36.6 1.8 %collective-permute-start.1 = (bf16[2,24,1024]{2,1,0:T(8,128)(2,1)S(1)}, bf16[2,24,1024]{2,1,0:T(8,128)(2,1)S(1)}, u32[]{:S(2)}, u32[]{:S(2)}) collective-permute-start(bf16[2,24,1024]{2,1,0:T(8,128)(2,1)S(1)} %shard_map.229.low), channel_id=1, source_target_pairs={{0,8},{1,9},{2,10},{3,11},{4,12},{5,13},{6,14},{7,15},{8,0},{9,1},... | collective-permute-start | bytes 294920 | tf_op jit(solution)/shard_map/ppermute | solution.py:607
  38.4 2.9 %collective-permute-done.1.high = bf16[2,24,1024]{2,1,0:T(8,128)(2,1)S(1)} collective-permute-done((bf16[2,24,1024]{2,1,0:T(8,128)(2,1)S(1)}, bf16[2,24,1024]{2,1,0:T(8,128)(2,1)S(1)}, u32[]{:S(2)}, u32[]{:S(2)}) %collective-permute-start.1) | collective-permute-done | bytes 98336 | tf_op jit(solution)/shard_map/ppermute | solution.py:607
  43.0 4.0 %collective-permute-done.2.high = bf16[4,24,1024]{2,1,0:T(8,128)(2,1)S(1)} collective-permute-done((bf16[4,24,1024]{2,1,0:T(8,128)(2,1)S(1)}, bf16[4,24,1024]{2,1,0:T(8,128)(2,1)S(1)}, u32[]{:S(2)}, u32[]{:S(2)}) %collective-permute-start.2) | collective-permute-done | bytes 196640 | tf_op jit(solution)/shard_map/ppermute | solution.py:607
  48.2 6.7 %collective-permute-done.3.high = bf16[8,24,1024]{2,1,0:T(8,128)(2,1)S(1)} collective-permute-done((bf16[8,24,1024]{2,1,0:T(8,128)(2,1)S(1)}, bf16[8,24,1024]{2,1,0:T(8,128)(2,1)S(1)}, u32[]{:S(2)}, u32[]{:S(2)}) %collective-permute-start.3) | collective-permute-done | bytes 393248 | tf_op jit(solution)/shard_map/ppermute | solution.py:607
  56.8 10.9 %shard_map.232 = (bf16[2,192,1024]{2,1,0:T(8,128)(2,1)S(1)}, bf16[2,576,1024]{2,1,0:T(8,128)(2,1)S(1)}, bf16[24,256,256]{2,1,0:T(8,128)(2,1)S(1)}, bf16[384,1024...) custom-call(s32[2]{0:T(128)S(1)} %pad_add_fusion.where, ...), custom_call_target="tpu_custom_call" | custom-call | flops 3000000000 | bytes 20000000 | tf_op jit(solution)/shard_map/pallas_call | solution.py:577
  67.8 22.0 %shard_map.236 = (bf16[1024,384]{1,0:T(8,128)(2,1)}, bf16[2048,384]{1,0:T(8,128)(2,1)}, bf16[2,192,1024]{2,1,0:T(8,128)(2,1)S(1)}, f32[384,1024]{1,0:T(8,128)S(1...) custom-call(s32[2]{0:T(128)S(1)} %pad_add_fusion.where, ...), custom_call_target="tpu_custom_call" | custom-call | flops 8000000000 | bytes 20000000 | tf_op jit(solution)/shard_map/pallas_call | solution.py:577
  90.3 3.3 %shard_map.237 = (bf16[2,576,256]{2,1,0:T(8,128)(2,1)S(1)}, f32[1,2,8,384]{3,2,1,0:T(8,128)S(1)}, bf16[1024,384]{1,0:T(8,128)(2,1)S(1)}, bf16[2048,384]{1,0:T(8,128)(2,1)}) custom-call(s32[2]{0:T(128)S(1)} %pad_add_fusion.where, bf16[2048,384]{1,0:T(8,128)(2,1)S(1)} %copy-done, f32[384,1024]{1,0:T(8,128)S(1)} %get-tuple-element.73.dx1_r, ...), custom_call_target="tpu_custom_call" | custom-call | flops 1500000000 | bytes 5000000 | tf_op jit(solution)/shard_map/pallas_call | solution.py:577
  94.3 8.2 %shard_map.238 = (bf16[2,576,768]{2,1,0:T(8,128)(2,1)S(1)}, f32[3,2,8,384]{3,2,1,0:T(8,128)S(1)}, bf16[1024,384]{1,0:T(8,128)(2,1)S(1)}, bf16[2048,384]{1,0:T(8,128)(2,1)}) custom-call(s32[2]{0:T(128)S(1)} %pad_add_fusion.where, bf16[2048,384]{1,0:T(8,128)(2,1)S(1)} %copy-done, ...), custom_call_target="tpu_custom_call", output_to_operand_aliasing={{2}: (8, {}), {3}: (9, {})} | custom-call | flops 4499999744 | bytes 5000000 | tf_op jit(solution)/shard_map/pallas_call | solution.py:577
  102.6 2.4 %shard_map.239 = (bf16[16,24,768]{2,1,0:T(8,128)(2,1)S(1)}, bf16[16,24,768]{2,1,0:T(8,128)(2,1)S(1)}, bf16[8,768]{1,0:T(8,128)(2,1)S(1)}, bf16[8,384]{1,0:T(8,128)(2,1)S(1)}) custom-call(s32[2]{0:T(128)S(1)} %pad_add_fusion.where, bf16[8,384]{1,0:T(8,128)(2,1)S(1)} %copy-done.3, bf16[384,1024]{1,0:T(8,128)(2,1)S(1)} %get-tuple-element.83.h1, ...), custom_call_target="tpu_custom_call" | custom-call | flops 1000000 | bytes 4000000 | tf_op jit(solution)/shard_map/pallas_call | solution.py:577
  106.5 2.4 %collective-permute-done.16.got_rows = bf16[8,768]{1,0:T(8,128)(2,1)S(1)} collective-permute-done((bf16[8,768]{1,0:T(8,128)(2,1)S(1)}, bf16[8,768]{1,0:T(8,128)(2,1)S(1)}, u32[]{:S(2)}, u32[]{:S(2)}) %collective-permute-start.16) | collective-permute-done | bytes 12320 | tf_op jit(solution)/shard_map/ppermute | solution.py:607
  111.9 6.5 %collective-permute-done.17.came = bf16[200,768]{1,0:T(8,128)(2,1)S(1)} collective-permute-done((bf16[200,768]{1,0:T(8,128)(2,1)S(1)}, bf16[200,768]{1,0:T(8,128)(2,1)S(1)}, u32[]{:S(2)}, u32[]{:S(2)}) %collective-permute-start.17) | collective-permute-done | bytes 307232 | tf_op jit(solution)/shard_map/ppermute | solution.py:607
  120.3 2.0 %collective-permute-start.25 = (bf16[48,2560]{1,0:T(8,128)(2,1)S(1)}, bf16[48,2560]{1,0:T(8,128)(2,1)S(1)}, u32[]{:S(2)}, u32[]{:S(2)}) collective-permute-start(bf16[48,2560]{1,0:T(8,128)(2,1)S(1)} %get-tuple-element.108), channel_id=1, source_target_pairs={{0,8},{1,9},{2,10},{3,11},{4,12},{5,13},{6,14},{7,15},{8,0},{9,1},... | collective-permute-start | bytes 737288 | tf_op jit(solution)/shard_map/ppermute | solution.py:607
  124.5 2.2 %collective-permute-start.23 = (bf16[48,1408]{1,0:T(8,128)(2,1)S(1)}, bf16[48,1408]{1,0:T(8,128)(2,1)S(1)}, u32[]{:S(2)}, u32[]{:S(2)}) collective-permute-start(bf16[48,1408]{1,0:T(8,128)(2,1)S(1)} %get-tuple-element.104), channel_id=1, source_target_pairs={{0,8},{1,9},{2,10},{3,11},{4,12},{5,13},{6,14},{7,15},{8,0},{9,1},... | collective-permute-start | bytes 405512 | tf_op jit(solution)/shard_map/ppermute | solution.py:607
  127.2 1.9 %collective-permute-done.25.came = bf16[48,2560]{1,0:T(8,128)(2,1)S(1)} collective-permute-done((bf16[48,2560]{1,0:T(8,128)(2,1)S(1)}, bf16[48,2560]{1,0:T(8,128)(2,1)S(1)}, u32[]{:S(2)}, u32[]{:S(2)}) %collective-permute-start.25) | collective-permute-done | bytes 245792 | tf_op jit(solution)/shard_map/ppermute | solution.py:607
  129.2 3.8 %collective-permute-start.26 = (bf16[24,2560]{1,0:T(8,128)(2,1)S(1)}, bf16[24,2560]{1,0:T(8,128)(2,1)S(1)}, u32[]{:S(2)}, u32[]{:S(2)}) collective-permute-start(bf16[24,2560]{1,0:T(8,128)(2,1)S(1)} %get-tuple-element.110), channel_id=1, source_target_pairs={{0,16},{1,17},{2,18},{3,19},{4,20},{5,21},{6,22},{7,23},{8,24},{9,... | collective-permute-start | bytes 368648 | tf_op jit(solution)/shard_map/ppermute | solution.py:607
  133.0 2.1 %constant_dynamic-update-slice_fusion.1 = bf16[2048,384]{1,0:T(8,128)(2,1)} fusion(bf16[2048,384]{1,0:T(8,128)(2,1)} %get-tuple-element.71, bf16[1024,384]{1,0:T(8,128)(2,1)} %collective-permute-done.12, s32[]{:T(128)S(6)} %select_n.4), kind=kLoop, calls=%fused_computation.3 | loop fusion | bytes 1572868 | tf_op jit(solution)/shard_map/dynamic_update_slice | solution.py:806
  135.8 3.8 %collective-permute-done.26.came = bf16[24,2560]{1,0:T(8,128)(2,1)S(1)} collective-permute-done((bf16[24,2560]{1,0:T(8,128)(2,1)S(1)}, bf16[24,2560]{1,0:T(8,128)(2,1)S(1)}, u32[]{:S(2)}, u32[]{:S(2)}) %collective-permute-start.26) | collective-permute-done | bytes 122912 | tf_op jit(solution)/shard_map/ppermute | solution.py:607
  (74 shorter events, 23.9 us)
Async XLA Ops:
  2.5 10.2 %collective-permute-start.6 = (bf16[1,24,2560]{2,1,0:T(8,128)(2,1)}, bf16[1,24,2560]{2,1,0:T(8,128)(2,1)S(1)}, u32[]{:S(2)}, u32[]{:S(2)}) collective-permute-start(bf16[1,24,2560]{2,1,0:T(8,128)(2,1)} %bitcast.16), channel_id=1, source_target_pairs={{0,16},{1,17},{2,18},{3,19},{4,20},{5,21},{6,22},{7,23},{8,24},{9,... | collective-permute-start | bytes 368648 | tf_op jit(solution)/shard_map/ppermute | solution.py:607
  13.7 7.2 %collective-permute-start.7 = (bf16[2,24,2560]{2,1,0:T(8,128)(2,1)S(1)}, bf16[2,24,2560]{2,1,0:T(8,128)(2,1)S(1)}, u32[]{:S(2)}, u32[]{:S(2)}) collective-permute-start(bf16[2,24,2560]{2,1,0:T(8,128)(2,1)S(1)} %shard_map.233.low), channel_id=1, source_target_pairs={{0,8},{1,9},{2,10},{3,11},{4,12},{5,13},{6,14},{7,15},{8,0},{9,1},... | collective-permute-start | bytes 737288 | tf_op jit(solution)/shard_map/ppermute | solution.py:607
  20.9 8.9 %collective-permute-start.8 = (bf16[4,24,2560]{2,1,0:T(8,128)(2,1)S(1)}, bf16[4,24,2560]{2,1,0:T(8,128)(2,1)S(1)}, u32[]{:S(2)}, u32[]{:S(2)}) collective-permute-start(bf16[4,24,2560]{2,1,0:T(8,128)(2,1)S(1)} %shard_map.234.low), channel_id=1, source_target_pairs={{0,4},{1,3},{2,6},{3,1},{4,0},{5,7},{6,2},{7,5},{8,12},{9,11},{10,... | collective-permute-start | bytes 1474568 | tf_op jit(solution)/shard_map/ppermute | solution.py:607
  29.9 17.9 %collective-permute-start.9 = (bf16[8,24,2560]{2,1,0:T(8,128)(2,1)S(1)}, bf16[8,24,2560]{2,1,0:T(8,128)(2,1)}, u32[]{:S(2)}, u32[]{:S(2)}) collective-permute-start(bf16[8,24,2560]{2,1,0:T(8,128)(2,1)S(1)} %shard_map.235.low), channel_id=1, source_target_pairs={{0,2},{1,5},{2,0},{3,7},{4,6},{5,1},{6,4},{7,3},{8,10},{9,13},{10,... | collective-permute-start | bytes 2949128 | tf_op jit(solution)/shard_map/ppermute | solution.py:607
  31.3 5.3 %collective-permute-start = (bf16[1,24,1024]{2,1,0:T(8,128)(2,1)S(1)}, bf16[1,24,1024]{2,1,0:T(8,128)(2,1)S(1)}, u32[]{:S(2)}, u32[]{:S(2)}) collective-permute-start(bf16[1,24,1024]{2,1,0:T(8,128)(2,1)S(1)} %bitcast.18), channel_id=1, source_target_pairs={{0,16},{1,17},{2,18},{3,19},{4,20},{5,21},{6,22},{7,23},{8,24},{9,... | collective-permute-start | bytes 147464 | tf_op jit(solution)/shard_map/ppermute | solution.py:607
  36.6 4.7 %collective-permute-start.1 = (bf16[2,24,1024]{2,1,0:T(8,128)(2,1)S(1)}, bf16[2,24,1024]{2,1,0:T(8,128)(2,1)S(1)}, u32[]{:S(2)}, u32[]{:S(2)}) collective-permute-start(bf16[2,24,1024]{2,1,0:T(8,128)(2,1)S(1)} %shard_map.229.low), channel_id=1, source_target_pairs={{0,8},{1,9},{2,10},{3,11},{4,12},{5,13},{6,14},{7,15},{8,0},{9,1},... | collective-permute-start | bytes 294920 | tf_op jit(solution)/shard_map/ppermute | solution.py:607
  41.3 5.7 %collective-permute-start.2 = (bf16[4,24,1024]{2,1,0:T(8,128)(2,1)S(1)}, bf16[4,24,1024]{2,1,0:T(8,128)(2,1)S(1)}, u32[]{:S(2)}, u32[]{:S(2)}) collective-permute-start(bf16[4,24,1024]{2,1,0:T(8,128)(2,1)S(1)} %shard_map.230.low), channel_id=1, source_target_pairs={{0,4},{1,3},{2,6},{3,1},{4,0},{5,7},{6,2},{7,5},{8,12},{9,11},{10,... | collective-permute-start | bytes 589832 | tf_op jit(solution)/shard_map/ppermute | solution.py:607
  47.1 7.8 %collective-permute-start.3 = (bf16[8,24,1024]{2,1,0:T(8,128)(2,1)S(1)}, bf16[8,24,1024]{2,1,0:T(8,128)(2,1)S(1)}, u32[]{:S(2)}, u32[]{:S(2)}) collective-permute-start(bf16[8,24,1024]{2,1,0:T(8,128)(2,1)S(1)} %shard_map.231.low), channel_id=1, source_target_pairs={{0,2},{1,5},{2,0},{3,7},{4,6},{5,1},{6,4},{7,3},{8,10},{9,13},{10,... | collective-permute-start | bytes 1179656 | tf_op jit(solution)/shard_map/ppermute | solution.py:607
  47.7 20.0 %collective-permute-start.10 = (bf16[8,24,2560]{2,1,0:T(8,128)(2,1)S(1)}, bf16[8,24,2560]{2,1,0:T(8,128)(2,1)}, u32[]{:S(2)}, u32[]{:S(2)}) collective-permute-start(bf16[8,24,2560]{2,1,0:T(8,128)(2,1)S(1)} %shard_map.235.low), channel_id=1, source_target_pairs={{0,1},{1,0},{2,3},{3,2},{4,5},{5,4},{6,7},{7,6},{8,9},{9,8},{10,11... | collective-permute-start | bytes 2949128 | tf_op jit(solution)/shard_map/ppermute | solution.py:607
  47.7 20.0 %collective-permute-start.11 = (bf16[8,24,2560]{2,1,0:T(8,128)(2,1)}, bf16[8,24,2560]{2,1,0:T(8,128)(2,1)}, u32[]{:S(2)}, u32[]{:S(2)}) collective-permute-start(bf16[8,24,2560]{2,1,0:T(8,128)(2,1)} %collective-permute-done.9.high), channel_id=1, source_target_pairs={{0,1},{1,0},{2,3},{3,2},{4,5},{5,4},{6,7},{7,6},{8,9},{9,8},{10,11... | collective-permute-start | bytes 2949128 | tf_op jit(solution)/shard_map/ppermute | solution.py:607
  48.2 6.8 %collective-permute-start.4 = (bf16[8,24,1024]{2,1,0:T(8,128)(2,1)S(1)}, bf16[8,24,1024]{2,1,0:T(8,128)(2,1)}, u32[]{:S(2)}, u32[]{:S(2)}) collective-permute-start(bf16[8,24,1024]{2,1,0:T(8,128)(2,1)S(1)} %shard_map.231.low), channel_id=1, source_target_pairs={{0,1},{1,0},{2,3},{3,2},{4,5},{5,4},{6,7},{7,6},{8,9},{9,8},{10,11... | collective-permute-start | bytes 1179656 | tf_op jit(solution)/shard_map/ppermute | solution.py:607
  89.8 3.8 %collective-permute-start.19 = (bf16[16,24,1792]{2,1,0:T(8,128)(2,1)S(1)}, bf16[16,24,1792]{2,1,0:T(8,128)(2,1)S(1)}, u32[]{:S(2)}, u32[]{:S(2)}) collective-permute-start(bf16[16,24,1792]{2,1,0:T(8,128)(2,1)S(1)} %get-tuple-element.97), channel_id=1, source_target_pairs={{0,1},{1,0},{2,3},{3,2},{4,5},{5,4},{6,7},{7,6},{8,9},{9,8},{10,11... | collective-permute-start | bytes 4128776 | tf_op jit(solution)/shard_map/ppermute | solution.py:607
  93.7 16.2 %collective-permute-start.21 = (bf16[200,1792]{1,0:T(8,128)(2,1)S(1)}, bf16[200,1792]{1,0:T(8,128)(2,1)S(1)}, u32[]{:S(2)}, u32[]{:S(2)}) collective-permute-start(bf16[200,1792]{1,0:T(8,128)(2,1)S(1)} %shard_map.242.sent), channel_id=1, source_target_pairs={{0,2},{1,5},{2,0},{3,7},{4,6},{5,1},{6,4},{7,3},{8,10},{9,13},{10,... | collective-permute-start | bytes 2150408 | tf_op jit(solution)/shard_map/ppermute | solution.py:607
  105.0 3.9 %collective-permute-start.15 = (bf16[16,24,768]{2,1,0:T(8,128)(2,1)S(1)}, bf16[16,24,768]{2,1,0:T(8,128)(2,1)S(1)}, u32[]{:S(2)}, u32[]{:S(2)}) collective-permute-start(bf16[16,24,768]{2,1,0:T(8,128)(2,1)S(1)} %get-tuple-element.92), channel_id=1, source_target_pairs={{0,1},{1,0},{2,3},{3,2},{4,5},{5,4},{6,7},{7,6},{8,9},{9,8},{10,11... | collective-permute-start | bytes 1769480 | tf_op jit(solution)/shard_map/ppermute | solution.py:607
  106.0 27.0 %collective-permute-start.12 = (bf16[1024,384]{1,0:T(8,128)(2,1)}, bf16[1024,384]{1,0:T(8,128)(2,1)}, u32[]{:S(2)}, u32[]{:S(2)}) collective-permute-start(bf16[1024,384]{1,0:T(8,128)(2,1)} %get-tuple-element.72), channel_id=1, source_target_pairs={{0,1},{1,0},{2,3},{3,2},{4,5},{5,4},{6,7},{7,6},{8,9},{9,8},{10,11... | collective-permute-start | bytes 2359304 | tf_op jit(solution)/shard_map/ppermute | solution.py:607
  109.0 9.4 %collective-permute-start.17 = (bf16[200,768]{1,0:T(8,128)(2,1)S(1)}, bf16[200,768]{1,0:T(8,128)(2,1)S(1)}, u32[]{:S(2)}, u32[]{:S(2)}) collective-permute-start(bf16[200,768]{1,0:T(8,128)(2,1)S(1)} %shard_map.240.sent), channel_id=1, source_target_pairs={{0,2},{1,5},{2,0},{3,7},{4,6},{5,1},{6,4},{7,3},{8,10},{9,13},{10,... | collective-permute-start | bytes 921608 | tf_op jit(solution)/shard_map/ppermute | solution.py:607
  110.0 31.1 %collective-permute-start.13 = (bf16[1024,384]{1,0:T(8,128)(2,1)S(1)}, bf16[1024,384]{1,0:T(8,128)(2,1)S(1)}, u32[]{:S(2)}, u32[]{:S(2)}) collective-permute-start(bf16[1024,384]{1,0:T(8,128)(2,1)S(1)} %get-tuple-element.82), channel_id=1, source_target_pairs={{0,1},{1,0},{2,3},{3,2},{4,5},{5,4},{6,7},{7,6},{8,9},{9,8},{10,11... | collective-permute-start | bytes 2359304 | tf_op jit(solution)/shard_map/ppermute | solution.py:607
  110.2 9.4 %collective-permute-start.22 = (bf16[112,1792]{1,0:T(8,128)(2,1)S(1)}, bf16[112,1792]{1,0:T(8,128)(2,1)S(1)}, u32[]{:S(2)}, u32[]{:S(2)}) collective-permute-start(bf16[112,1792]{1,0:T(8,128)(2,1)S(1)} %get-tuple-element.101.refs_1_), channel_id=1, source_target_pairs={{0,4},{1,3},{2,6},{3,1},{4,0},{5,7},{6,2},{7,5},{8,12},{9,11},{10,... | collective-permute-start | bytes 1204232 | tf_op jit(solution)/shard_map/ppermute | solution.py:607
  118.5 5.5 %collective-permute-start.18 = (bf16[112,768]{1,0:T(8,128)(2,1)S(1)}, bf16[112,768]{1,0:T(8,128)(2,1)S(1)}, u32[]{:S(2)}, u32[]{:S(2)}) collective-permute-start(bf16[112,768]{1,0:T(8,128)(2,1)S(1)} %get-tuple-element.95.refs_1_), channel_id=1, source_target_pairs={{0,4},{1,3},{2,6},{3,1},{4,0},{5,7},{6,2},{7,5},{8,12},{9,11},{10,... | collective-permute-start | bytes 516104 | tf_op jit(solution)/shard_map/ppermute | solution.py:607
  120.3 8.9 %collective-permute-start.25 = (bf16[48,2560]{1,0:T(8,128)(2,1)S(1)}, bf16[48,2560]{1,0:T(8,128)(2,1)S(1)}, u32[]{:S(2)}, u32[]{:S(2)}) collective-permute-start(bf16[48,2560]{1,0:T(8,128)(2,1)S(1)} %get-tuple-element.108), channel_id=1, source_target_pairs={{0,8},{1,9},{2,10},{3,11},{4,12},{5,13},{6,14},{7,15},{8,0},{9,1},... | collective-permute-start | bytes 737288 | tf_op jit(solution)/shard_map/ppermute | solution.py:607
  122.2 4.4 %collective-permute-start.14 = (bf16[8,384]{1,0:T(8,128)(2,1)S(1)}, bf16[8,384]{1,0:T(8,128)(2,1)S(1)}, u32[]{:S(2)}, u32[]{:S(2)}) collective-permute-start(bf16[8,384]{1,0:T(8,128)(2,1)S(1)} %get-tuple-element.90), channel_id=1, source_target_pairs={{0,1},{1,0},{2,3},{3,2},{4,5},{5,4},{6,7},{7,6},{8,9},{9,8},{10,11... | collective-permute-start | bytes 18440 | tf_op jit(solution)/shard_map/ppermute | solution.py:789
  124.5 10.6 %collective-permute-start.23 = (bf16[48,1408]{1,0:T(8,128)(2,1)S(1)}, bf16[48,1408]{1,0:T(8,128)(2,1)S(1)}, u32[]{:S(2)}, u32[]{:S(2)}) collective-permute-start(bf16[48,1408]{1,0:T(8,128)(2,1)S(1)} %get-tuple-element.104), channel_id=1, source_target_pairs={{0,8},{1,9},{2,10},{3,11},{4,12},{5,13},{6,14},{7,15},{8,0},{9,1},... | collective-permute-start | bytes 405512 | tf_op jit(solution)/shard_map/ppermute | solution.py:607
  129.2 10.5 %collective-permute-start.26 = (bf16[24,2560]{1,0:T(8,128)(2,1)S(1)}, bf16[24,2560]{1,0:T(8,128)(2,1)S(1)}, u32[]{:S(2)}, u32[]{:S(2)}) collective-permute-start(bf16[24,2560]{1,0:T(8,128)(2,1)S(1)} %get-tuple-element.110), channel_id=1, source_target_pairs={{0,16},{1,17},{2,18},{3,19},{4,20},{5,21},{6,22},{7,23},{8,24},{9,... | collective-permute-start | bytes 368648 | tf_op jit(solution)/shard_map/ppermute | solution.py:607
  135.1 6.1 %collective-permute-start.24 = (bf16[24,1408]{1,0:T(8,128)(2,1)S(1)}, bf16[24,1408]{1,0:T(8,128)(2,1)S(1)}, u32[]{:S(2)}, u32[]{:S(2)}) collective-permute-start(bf16[24,1408]{1,0:T(8,128)(2,1)S(1)} %get-tuple-element.106), channel_id=1, source_target_pairs={{0,16},{1,17},{2,18},{3,19},{4,20},{5,21},{6,22},{7,23},{8,24},{9,... | collective-permute-start | bytes 202760 | tf_op jit(solution)/shard_map/ppermute | solution.py:607
  (12 other events, 132.2 us)
